TPU v7x, 32 devices: a whole 2x2x4 slice. The times are simulated.
32 devices in a mesh: dp: 8 (over z, y), mp: 4 (over x, core).
Axes of the slice: x: 2, y: 2, z: 4, core: 2. Of those that a mesh axis runs over, the one named last changes fastest.
Arguments:
- hidden_in: bfloat16 [8192, 2048], P('dp', 'mp'), may hold values from -13 to 13
- cotangent: bfloat16 [8192, 2048], P('dp', 'mp'), may hold values from -6 to 6
- span_starts: int32 [32], P('dp'), may hold values from 0 to 1, as said below
- span_fill: int32 [32], P('dp'), may hold values from 128 to 256, as said below
- norm_gain: float32 [2048], replicated, may hold values from 0.5 to 1.5
- w_gate: bfloat16 [2048, 4096], P(None, 'mp'), may hold values from -0.125 to 0.125
- w_value: bfloat16 [2048, 4096], P(None, 'mp'), may hold values from -0.125 to 0.125
- w_select: bfloat16 [2048, 256], replicated, may hold values from -0.125 to 0.125
- w_step: bfloat16 [2048, 64], P(None, 'mp'), may hold values from -0.125 to 0.125
- conv_value: float32 [4, 4096], P(None, 'mp'), may hold values from -3 to 3
- conv_value_bias: float32 [4096], P('mp'), may hold values from -3 to 3
- conv_select: float32 [4, 256], replicated, may hold values from -3 to 3
- conv_select_bias: float32 [256], replicated, may hold values from -3 to 3
- step_bias: float32 [64], P('mp'), may hold values from -6 to -3
- decay_log: float32 [64], P('mp'), may hold values from 0 to 2.7
- skip_gain: float32 [64], P('mp'), may hold values from 0.5 to 1.5
- gate_gain: float32 [4096], P('mp'), may hold values from 0.5 to 1.5
- w_out: bfloat16 [4096, 2048], P('mp'), may hold values from -0.09375 to 0.09375
Outputs:
- output: bfloat16 [8192, 2048], P('dp', 'mp')
- grad_hidden_in: float32 [8192, 2048], P('dp', 'mp')
- grad_norm_gain: float32 [2048], P('mp')
- grad_w_gate: float32 [2048, 4096], P('dp', 'mp')
- grad_w_value: float32 [2048, 4096], P('dp', 'mp')
- grad_w_select: float32 [2048, 256], P('dp')
- grad_w_step: float32 [2048, 64], P('dp', 'mp')
- grad_conv_value: float32 [4, 4096], P(None, 'mp')
- grad_conv_value_bias: float32 [4096], P('mp')
- grad_conv_select: float32 [4, 256], replicated
- grad_conv_select_bias: float32 [256], replicated
- grad_step_bias: float32 [64], P('mp')
- grad_decay_log: float32 [64], P('mp')
- grad_skip_gain: float32 [64], P('mp')
- grad_gate_gain: float32 [4096], P('mp')
- grad_w_out: float32 [4096, 2048], P('mp', 'dp')
Inputs may be any that keep to these rules, and one draw needn't show every extreme that they name: `span_starts`: the first of every device's 1024 / 256 spans has 1; a sequence runs from a span with 1 to the span before the next one or to its device's last span; on some device a single sequence fills every span. `span_fill`: 256 in every span but the last one of a sequence; the real tokens come first in a span.
All inputs are finite; a program needn't handle non-finite values.
Results may differ from a plain program's by a relative error of at most 0.00205.
The roundings to bfloat16 on the way count: a program that leaves them out, or rounds other values in their place, can miss the bound.
Values may be sent and summed in bfloat16 or wider, within the bound.
No kernel may reach another device: no remote copies, remote signals or barrier semaphores. Data moves between devices by JAX's collectives and lax.ppermute only.
A program may use at most 192 MiB of HBM per device.

v0:
```python
import jax
import jax.numpy as jnp
from jax import lax
from jax.sharding import PartitionSpec as P

CONV = 4
SPAN = 256


exact_mode = lax.Precision.HIGHEST
epsilon = 1e-05


def layout(start_flags, fill_counts, token_rows):
    places = jnp.arange(token_rows) % SPAN
    fill_tokens = jnp.repeat(fill_counts, SPAN, total_repeat_length=token_rows)
    live_mask = (places < fill_tokens).astype(jnp.float32)
    seq_numbers = jnp.repeat(jnp.cumsum(start_flags), SPAN, total_repeat_length=token_rows)
    same_links = []
    for back_steps in range(1, CONV):
        earlier = jnp.concatenate(
            [jnp.full((back_steps,), -1, jnp.int32), seq_numbers[:-back_steps]]
        )
        same_links.append((earlier == seq_numbers).astype(jnp.float32))
    keep_flags = (1 - start_flags).astype(jnp.float32)
    return (live_mask, same_links, keep_flags)


def conv_silu(pre_act, kernel, bias_vec, same_links):
    running_sum = bias_vec[None, :] + kernel[CONV - 1][None, :] * pre_act
    for back_steps in range(1, CONV):
        shifted = jnp.concatenate(
            [jnp.zeros((back_steps, pre_act.shape[1]), jnp.float32), pre_act[:-back_steps]], axis=0
        )
        running_sum = (
            running_sum
            + kernel[CONV - 1 - back_steps][None, :] * shifted * same_links[back_steps - 1][:, None]
        )
    return jax.nn.silu(running_sum)


def scan_span(state, span_values, inflow, readout, step_sizes, decay_rates, skip_factor):
    length = span_values.shape[0]
    lower_mask = (jnp.arange(length)[:, None] >= jnp.arange(length)[None, :]).astype(jnp.float32)
    log_steps = (step_sizes * decay_rates[None, :]).T
    cumulative = jnp.dot(log_steps, lower_mask.T, precision=exact_mode)
    log_gaps = cumulative[:, :, None] - cumulative[:, None, :]
    weights = jnp.exp(jnp.where(lower_mask[None, :, :] > 0, log_gaps, 0.0)) * lower_mask[None, :, :]
    scores = jnp.dot(readout, inflow.T, precision=exact_mode)
    inputs = span_values * step_sizes[:, :, None]
    inner_part = jnp.einsum(
        "hts,shp->thp", scores[None, :, :] * weights, inputs, precision=exact_mode
    )
    carried = (
        jnp.einsum("tn,hpn->thp", readout, state, precision=exact_mode)
        * jnp.exp(cumulative).T[:, :, None]
    )
    outputs = inner_part + carried + skip_factor[None, :, None] * span_values
    tail_decay = jnp.exp(cumulative[:, -1:] - cumulative)
    fresh_state = jnp.einsum("hs,shp,sn->hpn", tail_decay, inputs, inflow, precision=exact_mode)
    new_state = jnp.exp(cumulative[:, -1])[:, None, None] * state + fresh_state
    return (outputs, new_state)


def contract_rows(left_arr, right_arr):
    return lax.dot_general(
        left_arr, right_arr, (((0,), (0,)), ((), ())), preferred_element_type=jnp.float32
    )


def contract_cols(left_arr, right_arr):
    return lax.dot_general(
        left_arr, right_arr, (((1,), (1,)), ((), ())), preferred_element_type=jnp.float32
    )


def on_device(
    hidden_in,
    cotangent,
    span_starts,
    span_fill,
    norm_gain,
    w_gate,
    w_value,
    w_select,
    w_step,
    conv_value,
    conv_value_bias,
    conv_select,
    conv_select_bias,
    step_bias,
    decay_log,
    skip_gain,
    gate_gain,
    w_out,
):
    token_rows = hidden_in.shape[0]
    model_width = norm_gain.shape[0]
    inner_cols = w_gate.shape[1]
    local_heads = w_step.shape[1]
    head_dim = inner_cols // local_heads
    state_dim = w_select.shape[1] // 2
    model_parts = lax.axis_size("mp")
    feature_piece = model_width // model_parts
    offset = lax.axis_index("mp") * feature_piece
    span_count = token_rows // SPAN
    live_mask, same_links, keep_flags = layout(span_starts, span_fill, token_rows)
    whole_in = lax.all_gather(hidden_in, "mp", axis=1, tiled=True).astype(jnp.float32)
    input_scale = lax.rsqrt(jnp.mean(whole_in * whole_in, axis=1, keepdims=True) + epsilon)
    normed = (whole_in * input_scale * norm_gain[None, :]).astype(jnp.bfloat16)
    gate_pre = jnp.dot(normed, w_gate, preferred_element_type=jnp.float32)
    value_pre = jnp.dot(normed, w_value, preferred_element_type=jnp.float32)
    step_pre = jnp.dot(normed, w_step, preferred_element_type=jnp.float32)
    select_pre = jnp.dot(normed, w_select, preferred_element_type=jnp.float32)
    value_act, value_pull = jax.vjp(
        lambda pre_act, kernel, bias_vec: conv_silu(pre_act, kernel, bias_vec, same_links),
        value_pre,
        conv_value,
        conv_value_bias,
    )
    select_act, select_pull = jax.vjp(
        lambda pre_act, kernel, bias_vec: conv_silu(pre_act, kernel, bias_vec, same_links),
        select_pre,
        conv_select,
        conv_select_bias,
    )
    values = lax.optimization_barrier(value_act.astype(jnp.bfloat16)).astype(jnp.float32)
    selects = lax.optimization_barrier(select_act.astype(jnp.bfloat16)).astype(jnp.float32)
    step_sizes, step_pull = jax.vjp(
        lambda pre_act, bias_vec: jax.nn.softplus(pre_act + bias_vec[None, :]) * live_mask[:, None],
        step_pre,
        step_bias,
    )
    decay_rates = -jnp.exp(decay_log)
    value_blocks = values.reshape(span_count, SPAN, local_heads, head_dim)
    inflow = selects[:, :state_dim].reshape(span_count, SPAN, state_dim)
    readout = selects[:, state_dim:].reshape(span_count, SPAN, state_dim)
    step_blocks = step_sizes.reshape(span_count, SPAN, local_heads)

    def advance(state_carry, span_items):
        keep_flag, span_values, span_inflow, span_readout, span_steps = span_items
        entering = state_carry * keep_flag
        outputs, leaving = scan_span(
            entering, span_values, span_inflow, span_readout, span_steps, decay_rates, skip_gain
        )
        return (leaving, (outputs, entering))

    start_state = jnp.zeros((local_heads, head_dim, state_dim), jnp.float32)
    _, (scanned, entered) = lax.scan(
        advance, start_state, (keep_flags, value_blocks, inflow, readout, step_blocks)
    )
    scan_flat = scanned.reshape(token_rows, inner_cols)
    gate_act = jax.nn.silu(gate_pre)
    gated_rows = live_mask[:, None] * scan_flat * gate_act
    square_sum = lax.psum(jnp.sum(gated_rows * gated_rows, axis=1), "mp")
    gate_scale = lax.rsqrt(square_sum[:, None] / (inner_cols * model_parts) + epsilon)
    scaled = (gated_rows * gate_scale * gate_gain[None, :]).astype(jnp.bfloat16)
    mixed_share = lax.psum_scatter(
        jnp.dot(scaled, w_out, preferred_element_type=jnp.float32),
        "mp",
        scatter_dimension=1,
        tiled=True,
    )
    own_in = hidden_in.astype(jnp.float32)
    output = (own_in + mixed_share).astype(jnp.bfloat16)
    whole_upstream = lax.all_gather(cotangent, "mp", axis=1, tiled=True)
    grad_out_local = contract_rows(scaled, whole_upstream)
    grad_scaled = contract_cols(whole_upstream, w_out)
    grad_gate_gain = jnp.sum(grad_scaled * gated_rows * gate_scale, axis=0)
    weighted = grad_scaled * gate_gain[None, :]
    gate_dot_sum = lax.psum(jnp.sum(weighted * gated_rows, axis=1), "mp")
    grad_gated = weighted * gate_scale - gated_rows * gate_scale**3 * gate_dot_sum[:, None] / (
        inner_cols * model_parts
    )
    grad_scan = grad_gated * live_mask[:, None] * gate_act
    sigmoid_gate = jax.nn.sigmoid(gate_pre)
    grad_gate = (
        grad_gated
        * live_mask[:, None]
        * scan_flat
        * sigmoid_gate
        * (1.0 + gate_pre * (1.0 - sigmoid_gate))
    ).astype(jnp.bfloat16)
    grad_blocks = grad_scan.reshape(span_count, SPAN, local_heads, head_dim)

    def retreat(back_carry, span_items):
        grad_state, grad_rates, grad_skip = back_carry
        keep_flag, entering, span_values, span_inflow, span_readout, span_steps, grad_outputs = (
            span_items
        )
        _, span_pull = jax.vjp(
            scan_span,
            entering,
            span_values,
            span_inflow,
            span_readout,
            span_steps,
            decay_rates,
            skip_gain,
        )
        back_enter, back_values, back_inflow, back_readout, back_steps, back_rates, back_skip = (
            span_pull((grad_outputs, grad_state))
        )
        return (
            (back_enter * keep_flag, grad_rates + back_rates, grad_skip + back_skip),
            (back_values, back_inflow, back_readout, back_steps),
        )

    back_start = (start_state, jnp.zeros_like(decay_rates), jnp.zeros_like(skip_gain))
    (_, grad_rates, grad_skip_gain), (back_values, back_inflow, back_readout, back_steps) = (
        lax.scan(
            retreat,
            back_start,
            (keep_flags, entered, value_blocks, inflow, readout, step_blocks, grad_blocks),
            reverse=True,
        )
    )
    grad_decay_log = grad_rates * decay_rates
    grad_values = back_values.reshape(token_rows, inner_cols)
    select_local = jnp.concatenate(
        [back_inflow.reshape(token_rows, state_dim), back_readout.reshape(token_rows, state_dim)],
        axis=1,
    )
    grad_selects = lax.psum(select_local, "mp")
    grad_value_pre, grad_conv_value, grad_conv_value_bias = value_pull(grad_values)
    grad_select_pre, grad_conv_select, grad_conv_select_bias = select_pull(grad_selects)
    grad_step_pre, grad_step_bias = step_pull(back_steps.reshape(token_rows, local_heads))
    grad_value_low = grad_value_pre.astype(jnp.bfloat16)
    grad_select_low = grad_select_pre.astype(jnp.bfloat16)
    grad_step_low = grad_step_pre.astype(jnp.bfloat16)
    normed_part = (
        contract_cols(grad_gate, w_gate)
        + contract_cols(grad_value_low, w_value)
        + contract_cols(grad_step_low, w_step)
    )
    select_rows = lax.dynamic_slice_in_dim(w_select, offset, feature_piece, 0)
    grad_normed = lax.psum_scatter(
        normed_part, "mp", scatter_dimension=1, tiled=True
    ) + contract_cols(grad_select_low, select_rows)
    own_gain = lax.dynamic_slice_in_dim(norm_gain, offset, feature_piece, 0)
    weighted_in = grad_normed * own_gain[None, :]
    norm_dot_sum = lax.psum(jnp.sum(weighted_in * own_in, axis=1), "mp")
    grad_hidden_in = (
        cotangent.astype(jnp.float32)
        + weighted_in * input_scale
        - own_in * input_scale**3 * norm_dot_sum[:, None] / model_width
    )
    grad_norm_gain = jnp.sum(grad_normed * own_in * input_scale, axis=0)
    grad_w_gate, grad_w_value, grad_w_step, grad_w_select = (
        lax.psum_scatter(contract_rows(normed, grad_gate), "dp", scatter_dimension=0, tiled=True),
        lax.psum_scatter(
            contract_rows(normed, grad_value_low), "dp", scatter_dimension=0, tiled=True
        ),
        lax.psum_scatter(
            contract_rows(normed, grad_step_low), "dp", scatter_dimension=0, tiled=True
        ),
        lax.psum_scatter(
            contract_rows(normed, grad_select_low), "dp", scatter_dimension=0, tiled=True
        ),
    )
    grad_w_out = lax.psum_scatter(grad_out_local, "dp", scatter_dimension=1, tiled=True)
    small_sums = lax.psum(
        (
            grad_norm_gain,
            grad_conv_value,
            grad_conv_value_bias,
            grad_conv_select,
            grad_conv_select_bias,
            grad_step_bias,
            grad_decay_log,
            grad_skip_gain,
            grad_gate_gain,
        ),
        "dp",
    )
    return (
        output,
        grad_hidden_in,
        small_sums[0],
        grad_w_gate,
        grad_w_value,
        grad_w_select,
        grad_w_step,
        small_sums[1],
        small_sums[2],
        small_sums[3],
        small_sums[4],
        small_sums[5],
        small_sums[6],
        small_sums[7],
        small_sums[8],
        grad_w_out,
    )


def solution(mesh):
    in_specs = (
        P("dp", "mp"),
        P("dp", "mp"),
        P("dp"),
        P("dp"),
        P(),
        P(None, "mp"),
        P(None, "mp"),
        P(),
        P(None, "mp"),
        P(None, "mp"),
        P("mp"),
        P(),
        P(),
        P("mp"),
        P("mp"),
        P("mp"),
        P("mp"),
        P("mp", None),
    )
    out_specs = (
        P("dp", "mp"),
        P("dp", "mp"),
        P("mp"),
        P("dp", "mp"),
        P("dp", "mp"),
        P("dp", None),
        P("dp", "mp"),
        P(None, "mp"),
        P("mp"),
        P(),
        P(),
        P("mp"),
        P("mp"),
        P("mp"),
        P("mp"),
        P("mp", "dp"),
    )
    return jax.shard_map(
        on_device, mesh=mesh, in_specs=in_specs, out_specs=out_specs, check_vma=False
    )
```

profile of v0, /device:TPU:0, one launch (start us, length us, event | category | flops | bytes accessed | tf_op | source)
XLA Modules:
  0.0 1186.7 jit_solution(15433164875659130069)
XLA Ops:
  24.1 22.8 %all-gather.3.cloned.1.call-done = bf16[1024,2048]{1,0:T(8,128)(2,1)} async-done(((bf16[1024,512]{1,0:T(8,128)(2,1)}), bf16[1024,2048]{1,0:T(8,128)(2,1)}) %all-gather.3.cloned.1.call-update) | async-done | bytes 4194320 | tf_op jit(solution)/shard_map/all_gather | solution.py:108
  69.9 7.7 copy.51
  88.3 69.8 %while.44 = (s32[]{:T(128)}, f32[16,64,128]{2,1,0:T(8,128)S(1)}, f32[4,256,16,64]{1,3,2,0:T(8,128)}, f32[4,16,64,128]{3,2,1,0:T(8,128)}, f32[4,256,16]{1,2,0:T(8...) while((s32[]{:T(128)}, f32[16,64,128]{2,1,0:T(8,128)S(1)}, ...), condition=%wide.region_3.5_spmd.clone, body=%wide.region_2.4_spmd.clone.sunk | while | flops 1731207168 | bytes 10837017 | solution.py:149
  89.2 7.0 fusion.292
  106.6 7.0 fusion.292
  141.4 7.0 fusion.292
  158.1 8.1 copy.77
  166.2 7.6 reshape.420
  173.8 12.7 %multiply_reduce_fusion.9 = (f32[1024]{0:T(1024)S(1)}, f32[1024,1024]{1,0:T(8,128)}, f32[1024,1024]{1,0:T(8,128)}) fusion(f32[1024,1024]{1,0:T(8,128)} %reshape.420, f32[1024]{0:T(1024)S(1)} %get-tuple-element.728, bf16[1024,2048]{1,0:T(8,128)(2,1)} %copy-done.5, bf16[2048,1024]{1,0:T(8,128)(2,1)} %param.33), kind=kOutput, calls=%fused_computation.210 | convolution fusion | flops 4303354880 | bytes 20979712 | tf_op jit(solution)/shard_map/dot_general | solution.py:111
  193.0 11.9 %multiply_reduce_fusion.3 = (f32[1024]{0:T(1024)}, f32[1024]{0:T(1024)S(1)}, f32[1024,1024]{1,0:T(8,128)}) fusion(f32[1024,1024]{1,0:T(8,128)} %get-tuple-element.680, f32[1024]{0:T(1024)S(1)} %get-tuple-element.720, f32[1024]{0:T(1024)S(1)} %copy-done.17, bf16[1024,2048]{1,0:T(8,128)(2,1)} %all-gather.5.cloned.1.call-done, bf16[1024,2048]{1,0:T(8,128)(2,1)} %param.45), kind=kOutput, calls=%fused_computation.200 | convolution fusion | flops 4301256704 | bytes 16793600 | tf_op jit(solution)/shard_map/dot_general | solution.py:72
  210.5 9.2 fusion.170
  219.7 7.2 reshape.418
  227.0 7.7 copy.60
  238.8 151.2 %while.45 = (s32[]{:T(128)}, f32[16,64,128]{2,1,0:T(8,128)S(1)}, f32[16]{0:T(128)}, f32[16]{0:T(128)}, f32[4,256,16,64]{1,3,2,0:T(8,128)}, /*index=5*/f32[4,256,...) while((s32[]{:T(128)}, f32[16,64,128]{2,1,0:T(8,128)S(1)}, ...), condition=%wide.region_19.21_spmd.clone, body=%wide.region_9.20_spmd.clone.sunk | while | flops 3973435392 | bytes 26901588 | solution.py:211
  252.0 7.7 fusion.317
  289.2 7.7 fusion.317
  327.0 7.7 fusion.317
  364.9 7.7 fusion.317
  392.4 8.1 copy.79
  400.5 7.7 reshape.421
  437.3 12.9 %fusion.192 = f32[1024,2048]{1,0:T(8,128)} fusion(bf16[1024,2048]{1,0:T(8,128)(2,1)} %param.45, f32[1024,1024]{1,0:T(8,128)} %get-tuple-element.680, f32[1024]{0:T(1024)S(1)} %copy-done.17, f32[1024]{0:T(1024)S(1)} %get-tuple-element.720), kind=kOutput, calls=%fused_computation.289 | convolution fusion | flops 4298113024 | bytes 16785408 | tf_op jit(solution)/shard_map/dot_general | solution.py:159
  463.1 10.7 fusion.211
  474.1 11.6 fusion.191
  485.7 10.7 fusion.210
  498.1 12.3 %reduce-scatter.10.cloned.1.call-done = f32[1024,512]{1,0:T(8,128)} async-done(((f32[1024,2048]{1,0:T(8,128)}), f32[1024,512]{1,0:T(8,128)}) %reduce-scatter.10.cloned.1.call-update) | async-done | bytes 2097168 | tf_op jit(solution)/shard_map/reduce_scatter | solution.py:237
  514.3 38.1 %all-reduce.24 = (f32[512]{0:T(512)}, f32[4,1024]{1,0:T(4,128)}, f32[1024]{0:T(1024)}, f32[4,256]{1,0:T(4,128)}, f32[256]{0:T(256)}, /*index=5*/f32[16]{0:T(128)}, f32[16]{0:T(128)}, f32[16]{0:T(128)}, f32[1024]{0:T(1024)}) all-reduce(f32[512]{0:T(512)S(1)} %get-tuple-element.594, ...), channel_id=1, replica_groups=mesh['dp'=8,'mp'=4] {'dp'}, use_global_device_ids=true, to_apply=%region_25.27 | all-reduce | flops 7984 | bytes 63872 | tf_op jit(solution)/shard_map/psum | solution.py:262
  558.5 26.2 %reduce-scatter.8.cloned.1.call-done = f32[1024,512]{1,0:T(8,128)} async-done(((f32[1024,2048]{1,0:T(8,128)}), f32[1024,512]{1,0:T(8,128)}) %reduce-scatter.8.cloned.1.call-update) | async-done | bytes 2097168 | tf_op jit(solution)/shard_map/reduce_scatter | solution.py:158
  588.5 61.6 %reduce-scatter.18.cloned.1.call-done = f32[256,16]{0,1:T(8,128)} async-done(((f32[2048,16]{0,1:T(8,128)}), f32[256,16]{0,1:T(8,128)}) %reduce-scatter.18.cloned.1.call-update) | async-done | bytes 16400 | tf_op jit(solution)/shard_map/reduce_scatter | solution.py:254
  650.2 71.4 %reduce-scatter.16.cloned.1.call-done = f32[256,256]{1,0:T(8,128)} async-done(((f32[2048,256]{1,0:T(8,128)}), f32[256,256]{1,0:T(8,128)}) %reduce-scatter.16.cloned.1.call-update) | async-done | bytes 262160 | tf_op jit(solution)/shard_map/reduce_scatter | solution.py:257
  721.5 152.7 %reduce-scatter.14.cloned.1.call-done = f32[256,1024]{1,0:T(8,128)} async-done(((f32[2048,1024]{1,0:T(8,128)}), f32[256,1024]{1,0:T(8,128)}) %reduce-scatter.14.cloned.1.call-update) | async-done | bytes 1048592 | tf_op jit(solution)/shard_map/reduce_scatter | solution.py:251
  874.3 152.6 %reduce-scatter.20.cloned.1.call-done = f32[1024,256]{1,0:T(8,128)} async-done(((f32[1024,2048]{1,0:T(8,128)}), f32[1024,256]{1,0:T(8,128)}) %reduce-scatter.20.cloned.1.call-update) | async-done | bytes 1048592 | tf_op jit(solution)/shard_map/reduce_scatter | solution.py:261
  1026.9 152.5 %reduce-scatter.12.cloned.1.call-done = f32[256,1024]{1,0:T(8,128)} async-done(((f32[2048,1024]{1,0:T(8,128)}), f32[256,1024]{1,0:T(8,128)}) %reduce-scatter.12.cloned.1.call-update) | async-done | bytes 1048592 | tf_op jit(solution)/shard_map/reduce_scatter | solution.py:250
  (379 shorter events, 293.4 us)
Async XLA Ops:
  7.2 70.4 %copy-start = (bf16[2048,256]{1,0:T(8,128)(2,1)S(1)}, bf16[2048,256]{1,0:T(8,128)(2,1)}, u32[]{:S(2)}) copy-start(bf16[2048,256]{1,0:T(8,128)(2,1)} %param.35) | copy-start | bytes 3145732
  7.2 43.5 %copy-start.37 = (f32[2048]{0:T(1024)S(1)}, f32[2048]{0:T(1024)}, u32[]{:S(2)}) copy-start(f32[2048]{0:T(1024)} %param.32) | copy-start | bytes 24580
  7.2 39.6 %all-gather.3.cloned.1.call-start = ((), (), s32[]{:S(2)}) async-start(), calls=%async_computation.7 | async-start | bytes 5242880 | tf_op jit(solution)/shard_map/all_gather | solution.py:108
  7.9 185.1 %all-gather.5.cloned.1.call-start = ((), (), s32[]{:S(2)}) async-start(), calls=%async_computation.9 | async-start | bytes 5242880 | tf_op jit(solution)/shard_map/all_gather | solution.py:166
  8.7 446.6 %all-reduce.27.cloned.1.call-start = ((), (), s32[]{:S(2)}) async-start(), calls=%async_computation.11 | async-start | bytes 2097152 | tf_op jit(solution)/shard_map/psum | solution.py:224
  13.1 44.2 %copy-start.28 = (f32[1,1024]{1,0:T(1,128)}, f32[1,1024]{1,0:T(1,128)S(1)}, u32[]{:S(2)}) copy-start(f32[1,1024]{1,0:T(1,128)S(1)} %get-tuple-element.713) | copy-start | bytes 12292
  13.2 44.2 %copy-start.30 = (f32[1,1024]{1,0:T(1,128)}, f32[1,1024]{1,0:T(1,128)S(1)}, u32[]{:S(2)}) copy-start(f32[1,1024]{1,0:T(1,128)S(1)} %get-tuple-element.715) | copy-start | bytes 12292
  13.2 44.2 %copy-start.32 = (f32[1,1024]{1,0:T(1,128)}, f32[1,1024]{1,0:T(1,128)S(1)}, u32[]{:S(2)}) copy-start(f32[1,1024]{1,0:T(1,128)S(1)} %get-tuple-element.714) | copy-start | bytes 12292
  13.2 44.2 %copy-start.34 = (f32[1,1024]{1,0:T(1,128)}, f32[1,1024]{1,0:T(1,128)S(1)}, u32[]{:S(2)}) copy-start(f32[1,1024]{1,0:T(1,128)S(1)} %get-tuple-element.716) | copy-start | bytes 12292
  14.0 67.1 %copy-start.38 = (f32[1,256]{1,0:T(1,128)}, f32[1,256]{1,0:T(1,128)S(1)}, u32[]{:S(2)}) copy-start(f32[1,256]{1,0:T(1,128)S(1)} %get-tuple-element.721) | copy-start | bytes 3076
  14.0 67.1 %copy-start.40 = (f32[1,256]{1,0:T(1,128)}, f32[1,256]{1,0:T(1,128)S(1)}, u32[]{:S(2)}) copy-start(f32[1,256]{1,0:T(1,128)S(1)} %get-tuple-element.723) | copy-start | bytes 3076
  14.0 67.1 %copy-start.42 = (f32[1,256]{1,0:T(1,128)}, f32[1,256]{1,0:T(1,128)S(1)}, u32[]{:S(2)}) copy-start(f32[1,256]{1,0:T(1,128)S(1)} %get-tuple-element.722) | copy-start | bytes 3076
  14.1 67.1 %copy-start.44 = (f32[1,256]{1,0:T(1,128)}, f32[1,256]{1,0:T(1,128)S(1)}, u32[]{:S(2)}) copy-start(f32[1,256]{1,0:T(1,128)S(1)} %get-tuple-element.724) | copy-start | bytes 3076
  24.0 57.1 %copy-start.20 = (f32[1024]{0:T(1024)}, f32[1024]{0:T(1024)S(1)}, u32[]{:S(2)}) copy-start(f32[1024]{0:T(1024)S(1)} %get-tuple-element.726) | copy-start | bytes 12292
  24.1 57.1 %copy-start.22 = (f32[1024]{0:T(1024)}, f32[1024]{0:T(1024)S(1)}, u32[]{:S(2)}) copy-start(f32[1024]{0:T(1024)S(1)} %get-tuple-element.727) | copy-start | bytes 12292
  173.8 19.2 %copy-start.17 = (f32[1024]{0:T(1024)S(1)}, f32[1024]{0:T(1024)}, u32[]{:S(2)}) copy-start(f32[1024]{0:T(1024)} %param.44) | copy-start | bytes 12292
  240.8 21.3 %copy-start.26 = (f32[16]{0:T(128)}, f32[16]{0:T(128)S(1)}, u32[]{:S(2)}) copy-start(f32[16]{0:T(128)S(1)} %get-tuple-element.939) | copy-start | bytes 196 | tf_op jit(solution)/shard_map/while
  277.9 21.4 %copy-start.26 = (f32[16]{0:T(128)}, f32[16]{0:T(128)S(1)}, u32[]{:S(2)}) copy-start(f32[16]{0:T(128)S(1)} %get-tuple-element.939) | copy-start | bytes 196 | tf_op jit(solution)/shard_map/while
  296.9 17.0 %copy-start.57 = (f32[16]{0:T(128)S(1)}, f32[16]{0:T(128)}, u32[]{:S(2)}) copy-start(f32[16]{0:T(128)} %copy-done.56) | copy-start | bytes 196 | tf_op jit(solution)/shard_map/while
  315.8 21.4 %copy-start.26 = (f32[16]{0:T(128)}, f32[16]{0:T(128)S(1)}, u32[]{:S(2)}) copy-start(f32[16]{0:T(128)S(1)} %get-tuple-element.939) | copy-start | bytes 196 | tf_op jit(solution)/shard_map/while
  334.8 17.0 %copy-start.57 = (f32[16]{0:T(128)S(1)}, f32[16]{0:T(128)}, u32[]{:S(2)}) copy-start(f32[16]{0:T(128)} %copy-done.56) | copy-start | bytes 196 | tf_op jit(solution)/shard_map/while
  353.6 21.4 %copy-start.26 = (f32[16]{0:T(128)}, f32[16]{0:T(128)S(1)}, u32[]{:S(2)}) copy-start(f32[16]{0:T(128)S(1)} %get-tuple-element.939) | copy-start | bytes 196 | tf_op jit(solution)/shard_map/while
  392.3 118.1 %reduce-scatter.10.cloned.1.call-start = ((), (), s32[]{:S(2)}) async-start(), calls=%async_computation.10 | async-start | bytes 10485760 | tf_op jit(solution)/shard_map/reduce_scatter | solution.py:237
  437.2 147.6 %reduce-scatter.8.cloned.1.call-start = ((), (), s32[]{:S(2)}) async-start(), calls=%async_computation.8 | async-start | bytes 10485760 | tf_op jit(solution)/shard_map/reduce_scatter | solution.py:158
  450.2 199.9 %reduce-scatter.18.cloned.1.call-start = ((), (), s32[]{:S(2)}) async-start(), calls=%async_computation.15 | async-start | bytes 147456 | tf_op jit(solution)/shard_map/reduce_scatter | solution.py:254
  455.3 266.3 %reduce-scatter.16.cloned.1.call-start = ((), (), s32[]{:S(2)}) async-start(), calls=%async_computation.14 | async-start | bytes 2359296 | tf_op jit(solution)/shard_map/reduce_scatter | solution.py:257
  463.0 411.3 %reduce-scatter.14.cloned.1.call-start = ((), (), s32[]{:S(2)}) async-start(), calls=%async_computation.13 | async-start | bytes 9437184 | tf_op jit(solution)/shard_map/reduce_scatter | solution.py:251
  473.8 553.2 %reduce-scatter.20.cloned.1.call-start = ((), (), s32[]{:S(2)}) async-start(), calls=%async_computation.16 | async-start | bytes 9437184 | tf_op jit(solution)/shard_map/reduce_scatter | solution.py:261
  485.6 693.8 %reduce-scatter.12.cloned.1.call-start = ((), (), s32[]{:S(2)}) async-start(), calls=%async_computation.12 | async-start | bytes 9437184 | tf_op jit(solution)/shard_map/reduce_scatter | solution.py:250
  496.4 17.8 %copy-start.46 = (f32[1024]{0:T(1024)S(1)}, f32[1024]{0:T(1024)}, u32[]{:S(2)}) copy-start(f32[1024]{0:T(1024)} %get-tuple-element.590) | copy-start | bytes 12292
  496.5 88.3 %copy-start.12 = (bf16[1024,512]{1,0:T(8,128)(2,1)S(1)}, bf16[1024,512]{1,0:T(8,128)(2,1)}, u32[]{:S(2)}) copy-start(bf16[1024,512]{1,0:T(8,128)(2,1)} %param.29) | copy-start | bytes 3145732
  496.5 88.3 %copy-start.36 = (f32[1024]{0:T(1024)S(1)}, f32[1024]{0:T(1024)}, u32[]{:S(2)}) copy-start(f32[1024]{0:T(1024)} %get-tuple-element.717) | copy-start | bytes 12292
  (54 other events, 312.6 us)
Sparse Core Ops, SparseCore 0:
  9.6 37.1 all-gather.2
  48.4 34.4 all-gather.4
  392.4 37.4 all-reduce.26
  437.3 73.0 reduce-scatter.9
  512.8 71.8 reduce-scatter.7
  588.9 61.2 reduce-scatter.17
  654.7 66.8 reduce-scatter.15
  726.2 148.0 reduce-scatter.13
  878.5 148.3 reduce-scatter.19
  1031.4 147.9 reduce-scatter.11
where the time goes:
time: 1200 us; the launch traced here: 1190 us
  waiting for transfers between devices  654 us (54%)
  matrix products  290 us (24%)
  other arithmetic  85.6 us (7%)
  local copies, waits for them, and re-layouts  82.8 us (7%)
  blocking collectives  56.3 us (5%)
  between operations  15.4 us (1%)
    reduce_scatter x1, waiting for transfers between devices, on_device(): lax.psum_scatter(contract_rows(normed, grad_value_low), 'dp', scatter_dim...  153 us
    reduce_scatter x1, waiting for transfers between devices, on_device(): lax.psum_scatter(grad_out_local, 'dp', scatter_dimension=1, tiled=True)  153 us
    reduce_scatter x1, waiting for transfers between devices, on_device(): lax.psum_scatter(contract_rows(normed, grad_gate), 'dp', scatter_dimensio...  153 us
    dot_general x12, matrix products, scan_span(): jnp.einsum('hts,shp->thp', scores[None, :, :] * weights, inputs, precisio...  82.2 us
    reduce_scatter x1, waiting for transfers between devices, on_device(): lax.psum_scatter(contract_rows(normed, grad_select_low), 'dp', scatter_di...  71.4 us
    reduce_scatter x1, waiting for transfers between devices, on_device(): lax.psum_scatter(contract_rows(normed, grad_step_low), 'dp', scatter_dime...  61.6 us
    dot_general x16, matrix products, scan_span(): jnp.einsum('tn,hpn->thp', readout, state, precision=exact_mode)  51.3 us
    dot_general x5, matrix products, contract_rows(): lax.dot_general(left_arr, right_arr, (((0,), (0,)), ((), ())), preferred_...  40.3 us
  transfers between devices with their start and end apart: 10, of which 8 were waited for; matrix products, arithmetic and copies ran while one was open for 22% of the time, Pallas kernels for 0%

commit v1 on v0

v1 whole, which is shorter than its diff:
```python
import functools

import jax
import jax.numpy as jnp
from jax import lax
from jax.experimental import pallas as pl
from jax.experimental.pallas import tpu as pltpu
from jax.sharding import PartitionSpec as P

CONV = 4
SPAN = 256
LANES = 128
EXTRA = 8
TOP = 15.0
FAR = -1e30
epsilon = 1e-05
exact_mode = lax.Precision.HIGHEST


def settings(mebibytes, axes=1):
    return pltpu.CompilerParams(
        dimension_semantics=("arbitrary",) * axes, vmem_limit_bytes=mebibytes << 20
    )


def scalars():
    return pl.BlockSpec(memory_space=pltpu.SMEM)


def fixed(shape):
    return pl.BlockSpec(shape, lambda *_: (0,) * len(shape))


def split_bits(value):
    high = value.astype(jnp.bfloat16)
    low = (value - high.astype(jnp.float32)).astype(jnp.bfloat16)
    return high, low


def dot(left, right):
    return lax.dot_general(left, right, (((1,), (0,)), ((), ())), preferred_element_type=jnp.float32)


def dot_lanes(left, right):
    return lax.dot_general(left, right, (((1,), (1,)), ((), ())), preferred_element_type=jnp.float32)


def dot_rows(left, right):
    return lax.dot_general(left, right, (((0,), (0,)), ((), ())), preferred_element_type=jnp.float32)


def exact(left, right):
    return jnp.dot(left, right, precision=exact_mode, preferred_element_type=jnp.float32)


def beside(*pieces):
    return jnp.concatenate(pieces, axis=1)


def above(*pieces):
    return jnp.concatenate(pieces, axis=0)


def sigmoid(value):
    return 1.0 / (1.0 + jnp.exp(-value))


def iota(shape, axis):
    return lax.broadcasted_iota(jnp.int32, shape, axis)


def two_heads(columns, pair, in_first):
    first = columns[:, 2 * pair : 2 * pair + 1]
    second = columns[:, 2 * pair + 1 : 2 * pair + 2]
    return jnp.where(in_first, first, second)


def row_of(columns):
    return jnp.sum(jnp.transpose(columns), axis=0, keepdims=True)


def live_rows(fill, width):
    return (iota((SPAN, width), 0) < fill).astype(jnp.float32)


def norm_kernel(side, hidden, gain, normed_out, split_out, scale_out, *, piece):
    block = hidden[...].astype(jnp.float32)
    scale = lax.rsqrt(jnp.mean(block * block, axis=1, keepdims=True) + epsilon)
    normed = (block * scale * gain[...]).astype(jnp.bfloat16)
    normed_out[...] = normed
    scale_out[...] = jnp.broadcast_to(scale, scale_out.shape)
    store_split(side, normed, split_out, piece)


def store_split(side, block, split_out, piece):
    for index in range(block.shape[1] // piece):
        slot = jnp.where(side[0] == index % 2, 1, 0)
        start = index // 2 * piece
        split_out[pl.ds(slot, 1), :, start : start + piece] = block[
            None, :, index * piece : (index + 1) * piece
        ]


def split_kernel(side, block, split_out, *, piece):
    store_split(side, block[...], split_out, piece)


def normalize(hidden, gain, side, piece):
    rows, width = hidden.shape
    return pl.pallas_call(
        functools.partial(norm_kernel, piece=piece),
        grid=(rows // SPAN,),
        in_specs=[
            scalars(),
            pl.BlockSpec((SPAN, width), lambda i: (i, 0)),
            fixed((1, width)),
        ],
        out_specs=[
            pl.BlockSpec((SPAN, width), lambda i: (i, 0)),
            pl.BlockSpec((2, SPAN, width // 2), lambda i: (0, i, 0)),
            pl.BlockSpec((SPAN, LANES), lambda i: (i, 0)),
        ],
        out_shape=[
            jax.ShapeDtypeStruct((rows, width), jnp.bfloat16),
            jax.ShapeDtypeStruct((2, rows, width // 2), jnp.bfloat16),
            jax.ShapeDtypeStruct((rows, LANES), jnp.float32),
        ],
        compiler_params=settings(32),
        name="norm",
    )(side, hidden, gain)


def split_columns(array, side, piece):
    rows, width = array.shape
    return pl.pallas_call(
        functools.partial(split_kernel, piece=piece),
        grid=(rows // SPAN,),
        in_specs=[scalars(), pl.BlockSpec((SPAN, width), lambda i: (i, 0))],
        out_specs=pl.BlockSpec((2, SPAN, width // 2), lambda i: (0, i, 0)),
        out_shape=jax.ShapeDtypeStruct((2, rows, width // 2), array.dtype),
        compiler_params=settings(32),
        name="split",
    )(side, array)


def conv_of(extended, kernel, bias, lanes):
    total = bias[:, lanes]
    for back in range(CONV):
        tap = kernel[CONV - 1 - back : CONV - back, lanes]
        total = total + tap * extended[EXTRA - back : EXTRA - back + SPAN, lanes]
    return total


def forward_kernel(
    starts,
    fills,
    value_pre,
    gate_pre,
    grad_scaled,
    select_pre,
    step_pre,
    conv_value,
    conv_value_bias,
    conv_select,
    conv_select_bias,
    step_bias,
    decay_log,
    skip,
    gain,
    values_out,
    selects_out,
    scan_out,
    delta_out,
    sum_out,
    state_out,
    rows_out,
    extended,
    extended_select,
    state,
):
    step = pl.program_id(0)
    fresh = starts[step] == 1
    width = value_pre.shape[1]
    state_dim = select_pre.shape[1] // 2

    @pl.when(fresh)
    def _():
        extended[:EXTRA, :] = jnp.zeros((EXTRA, width), jnp.float32)
        extended_select[:EXTRA, :] = jnp.zeros((EXTRA, 2 * state_dim), jnp.float32)
        state[...] = jnp.zeros(state.shape, jnp.float32)

    @pl.when(jnp.logical_not(fresh))
    def _():
        extended[:EXTRA, :] = extended[SPAN:, :]
        extended_select[:EXTRA, :] = extended_select[SPAN:, :]

    extended[EXTRA:, :] = value_pre[...]
    extended_select[EXTRA:, :] = select_pre[...]
    state_out[0] = state[...]

    live = live_rows(fills[step], LANES)
    pre_step = step_pre[...] + step_bias[...]
    delta = live * (jnp.maximum(pre_step, 0.0) + jnp.log1p(jnp.exp(-jnp.abs(pre_step))))
    rate = -jnp.exp(decay_log[...])
    lower = (iota((SPAN, SPAN), 0) >= iota((SPAN, SPAN), 1)).astype(jnp.float32)
    cumulative = exact(lower, delta * rate)
    delta_out[...] = delta
    sum_out[...] = cumulative
    sums_across = jnp.transpose(cumulative)
    delta_across = jnp.transpose(delta)
    grown = jnp.exp(cumulative)
    tail = delta * jnp.exp(cumulative[SPAN - 1 : SPAN, :] - cumulative)

    halves = []
    for half in range(2):
        lanes = slice(half * state_dim, (half + 1) * state_dim)
        mixed = conv_of(extended_select, conv_select, conv_select_bias, lanes)
        chosen = (mixed * sigmoid(mixed)).astype(jnp.bfloat16)
        selects_out[:, lanes] = chosen
        halves.append(chosen)
    inflow, readout = halves
    inflow_across = jnp.transpose(inflow.astype(jnp.float32)).astype(jnp.bfloat16)
    scores = dot_lanes(readout, inflow)
    past = iota((SPAN, SPAN), 0) >= iota((SPAN, SPAN), 1)
    in_first = iota((SPAN, LANES), 1) < LANES // 2
    row_first = iota((1, LANES), 1) < LANES // 2
    readout_twice = beside(readout, readout)
    squares = jnp.zeros((SPAN, LANES), jnp.float32)
    products = jnp.zeros((SPAN, LANES), jnp.float32)
    for pair in range(width // LANES):
        lanes = slice(pair * LANES, (pair + 1) * LANES)
        mixed = conv_of(extended, conv_value, conv_value_bias, lanes)
        value_low = (mixed * sigmoid(mixed)).astype(jnp.bfloat16)
        values_out[:, lanes] = value_low
        value = value_low.astype(jnp.float32)
        entering = state[:, lanes]
        scan = dot(readout_twice, above(*split_bits(entering))) * two_heads(grown, pair, in_first)
        scan = scan + skip[:, lanes] * value
        for which in range(2):
            head = 2 * pair + which
            gaps = cumulative[:, head : head + 1] - sums_across[head : head + 1, :]
            weights = jnp.exp(jnp.where(past, gaps, FAR))
            mixing = scores * weights * delta_across[head : head + 1, :]
            own = jnp.where(in_first == (which == 0), value_low, jnp.zeros_like(value_low))
            high, low = split_bits(mixing)
            scan = scan + dot(high, own) + dot(low, own)
        scan_out[:, lanes] = scan
        gate = gate_pre[:, lanes]
        gated = live * scan * gate * sigmoid(gate)
        squares = squares + gated * gated
        products = products + grad_scaled[:, lanes] * gain[:, lanes] * gated
        weighted = value * two_heads(tail, pair, in_first)
        high, low = split_bits(weighted)
        last = two_heads(grown[SPAN - 1 : SPAN, :], pair, row_first)
        state[:, lanes] = entering * last + dot(inflow_across, high) + dot(inflow_across, low)
    rows_out[...] = above(row_of(squares), row_of(products), jnp.zeros((6, SPAN), jnp.float32))


def run_forward(starts, fills, tiles, vectors):
    value_pre, gate_pre, grad_scaled, select_pre, step_pre = tiles
    rows, width = value_pre.shape
    spans = rows // SPAN
    select_width = select_pre.shape[1]

    def tile(columns):
        return pl.BlockSpec((SPAN, columns), lambda i: (i, 0))

    def like(columns, dtype):
        return jax.ShapeDtypeStruct((rows, columns), dtype)

    return pl.pallas_call(
        forward_kernel,
        grid=(spans,),
        in_specs=[scalars(), scalars()]
        + [tile(array.shape[1]) for array in tiles]
        + [fixed(array.shape) for array in vectors],
        out_specs=[
            tile(width),
            tile(select_width),
            tile(width),
            tile(LANES),
            tile(LANES),
            pl.BlockSpec((1, select_width // 2, width), lambda i: (i, 0, 0)),
            pl.BlockSpec((8, SPAN), lambda i: (0, i)),
        ],
        out_shape=[
            like(width, jnp.bfloat16),
            like(select_width, jnp.bfloat16),
            like(width, jnp.float32),
            like(LANES, jnp.float32),
            like(LANES, jnp.float32),
            jax.ShapeDtypeStruct((spans, select_width // 2, width), jnp.float32),
            jax.ShapeDtypeStruct((8, rows), jnp.float32),
        ],
        scratch_shapes=[
            pltpu.VMEM((SPAN + EXTRA, width), jnp.float32),
            pltpu.VMEM((SPAN + EXTRA, select_width), jnp.float32),
            pltpu.VMEM((select_width // 2, width), jnp.float32),
        ],
        compiler_params=settings(48),
        name="forward",
    )(starts, fills, *tiles, *vectors)


def gate_kernel(
    fills,
    gate_pre,
    scan_in,
    grad_scaled,
    sums,
    gain,
    scaled_out,
    gate_out,
    scan_out,
    rows_out,
    stat_out,
    *,
    total_width,
):
    step = pl.program_id(0)
    width = gate_pre.shape[1]
    live = live_rows(fills[step], LANES)
    turned = jnp.transpose(above(sums[...], jnp.zeros((LANES - 8, SPAN), jnp.float32)))
    scale = lax.rsqrt(turned[:, 0:1] / total_width + epsilon)
    pull = scale * scale * scale * turned[:, 1:2] / total_width
    scale = jnp.broadcast_to(scale, (SPAN, LANES))
    pull = jnp.broadcast_to(pull, (SPAN, LANES))

    @pl.when(step == 0)
    def _():
        stat_out[...] = jnp.zeros(stat_out.shape, jnp.float32)

    dots = jnp.zeros((SPAN, LANES), jnp.float32)
    for pair in range(width // LANES):
        lanes = slice(pair * LANES, (pair + 1) * LANES)
        gate = gate_pre[:, lanes]
        scan = scan_in[:, lanes]
        upstream = grad_scaled[:, lanes]
        sig = sigmoid(gate)
        opened = live * gate * sig
        gated = scan * opened
        own_gain = gain[:, lanes]
        shrunk = gated * scale
        scaled_out[:, lanes] = (shrunk * own_gain).astype(jnp.bfloat16)
        grad_gated = upstream * own_gain * scale - gated * pull
        scan_out[:, lanes] = grad_gated * opened
        grad_gate = (grad_gated * live * scan * sig * (1.0 + gate * (1.0 - sig))).astype(jnp.bfloat16)
        gate_out[:, lanes] = grad_gate
        wide = grad_gate.astype(jnp.float32)
        dots = dots + wide * gate
        stat_out[0:1, lanes] += jnp.sum(upstream * shrunk, axis=0, keepdims=True)
        stat_out[1:2, lanes] = jnp.maximum(
            stat_out[1:2, lanes], jnp.max(jnp.abs(wide), axis=0, keepdims=True)
        )
    rows_out[...] = above(row_of(dots), jnp.zeros((7, SPAN), jnp.float32))


def run_gate(fills, gate_pre, scan, grad_scaled, sums, gain, total_width):
    rows, width = gate_pre.shape
    tile = pl.BlockSpec((SPAN, width), lambda i: (i, 0))
    strip = pl.BlockSpec((8, SPAN), lambda i: (0, i))
    return pl.pallas_call(
        functools.partial(gate_kernel, total_width=total_width),
        grid=(rows // SPAN,),
        in_specs=[scalars(), tile, tile, tile, strip, fixed((1, width))],
        out_specs=[tile, tile, tile, strip, fixed((8, width))],
        out_shape=[
            jax.ShapeDtypeStruct((rows, width), jnp.bfloat16),
            jax.ShapeDtypeStruct((rows, width), jnp.bfloat16),
            jax.ShapeDtypeStruct((rows, width), jnp.float32),
            jax.ShapeDtypeStruct((8, rows), jnp.float32),
            jax.ShapeDtypeStruct((8, width), jnp.float32),
        ],
        compiler_params=settings(40),
        name="gate",
    )(fills, gate_pre, scan, grad_scaled, sums, gain)


def backward_kernel(
    starts,
    fills,
    grad_scan,
    scan_in,
    values_in,
    value_pre,
    value_before,
    selects_in,
    delta_in,
    sum_in,
    step_pre,
    state_in,
    conv_value,
    conv_value_bias,
    step_bias,
    decay_log,
    skip,
    value_out,
    select_out,
    step_out,
    rows_out,
    stat_out,
    small_out,
    extended,
    shifted,
    state,
    carried,
    *,
    spans,
):
    step = pl.program_id(0)
    span = spans - 1 - step
    width = values_in.shape[1]
    state_dim = selects_in.shape[1] // 2
    following = jnp.minimum(span + 1, spans - 1)
    joined = jnp.logical_and(step > 0, starts[following] == 0)

    @pl.when(jnp.logical_not(joined))
    def _():
        shifted[SPAN:, :] = jnp.zeros((EXTRA, width), jnp.float32)
        state[...] = jnp.zeros(state.shape, jnp.float32)
        carried[...] = jnp.zeros(carried.shape, jnp.float32)

    @pl.when(joined)
    def _():
        shifted[SPAN:, :] = shifted[:EXTRA, :]

    @pl.when(step == 0)
    def _():
        stat_out[...] = jnp.zeros(stat_out.shape, jnp.float32)
        small_out[...] = jnp.zeros(small_out.shape, jnp.float32)

    fresh = starts[span] == 1

    @pl.when(fresh)
    def _():
        extended[:EXTRA, :] = jnp.zeros((EXTRA, width), jnp.float32)

    @pl.when(jnp.logical_not(fresh))
    def _():
        extended[:EXTRA, :] = value_before[...]

    extended[EXTRA:, :] = value_pre[...]

    delta = delta_in[...]
    cumulative = sum_in[...]
    sums_across = jnp.transpose(cumulative)
    grown = jnp.exp(cumulative)
    tail = jnp.exp(cumulative[SPAN - 1 : SPAN, :] - cumulative)
    delta_tail = delta * tail
    inflow = selects_in[:, :state_dim]
    readout = selects_in[:, state_dim:]
    readout_across = jnp.transpose(readout.astype(jnp.float32)).astype(jnp.bfloat16)
    scores = dot_lanes(inflow, readout)
    ahead = iota((SPAN, SPAN), 1) >= iota((SPAN, SPAN), 0)
    in_first = iota((SPAN, LANES), 1) < LANES // 2
    row_first = iota((1, LANES), 1) < LANES // 2
    inflow_twice = beside(inflow, inflow)
    grad_scores = jnp.zeros((SPAN, SPAN), jnp.float32)
    grad_inflow = jnp.zeros((SPAN, state_dim), jnp.float32)
    grad_readout = jnp.zeros((SPAN, state_dim), jnp.float32)
    change = jnp.zeros((SPAN, LANES), jnp.float32)
    direct = jnp.zeros((SPAN, LANES), jnp.float32)
    jump = jnp.zeros((8, LANES), jnp.float32)
    dots = jnp.zeros((SPAN, LANES), jnp.float32)
    for pair in range(width // LANES):
        lanes = slice(pair * LANES, (pair + 1) * LANES)
        upstream = grad_scan[:, lanes]
        up_high, up_low = split_bits(upstream)
        value_low = values_in[:, lanes]
        value = value_low.astype(jnp.float32)
        own_skip = skip[:, lanes]
        arriving = state[:, lanes]
        arriving_high, arriving_low = split_bits(arriving)
        entering = state_in[0, :, lanes]
        entering_high, entering_low = split_bits(entering)
        pulled = dot(inflow_twice, above(arriving_high, arriving_low)) * two_heads(tail, pair, in_first)
        up_both = beside(up_high, up_low)
        for which in range(2):
            head = 2 * pair + which
            mine = in_first == (which == 0)
            nothing = jnp.zeros_like(value_low)
            gaps = sums_across[head : head + 1, :] - cumulative[:, head : head + 1]
            weights = jnp.exp(jnp.where(ahead, gaps, FAR))
            high, low = split_bits(scores * weights)
            own_high = jnp.where(mine, up_high, nothing)
            own_low = jnp.where(mine, up_low, nothing)
            pulled = pulled + dot(high, own_high) + dot(high, own_low) + dot(low, own_high)
            own_value = jnp.where(mine, value_low, nothing)
            outer = dot_lanes(beside(own_value, own_value), up_both)
            grad_scores = grad_scores + outer * weights * delta[:, head : head + 1]
        delta_both = two_heads(delta, pair, in_first)
        grad_value = own_skip * upstream + delta_both * pulled
        pull_value = value * pulled
        spread = (
            iota((LANES, LANES), 1) == 2 * pair + iota((LANES, LANES), 0) // (LANES // 2)
        ).astype(jnp.bfloat16)
        spread_twice = above(spread, spread)
        moved = upstream * (scan_in[:, lanes] - own_skip * value) - delta_both * pull_value
        change = change + dot(beside(*split_bits(moved)), spread_twice)
        direct = direct + dot(beside(*split_bits(pull_value)), spread_twice)
        grown_up = upstream * two_heads(grown, pair, in_first)
        high, low = split_bits(grown_up)
        grad_readout = grad_readout + dot_lanes(
            beside(high, low, high), beside(entering_high, entering_high, entering_low)
        )
        last = two_heads(grown[SPAN - 1 : SPAN, :], pair, row_first)
        leaving = arriving * last + dot(readout_across, high) + dot(readout_across, low)
        tail_value = value * two_heads(delta_tail, pair, in_first)
        high, low = split_bits(tail_value)
        grad_inflow = grad_inflow + dot_lanes(
            beside(high, low, high), beside(arriving_high, arriving_high, arriving_low)
        )
        jump = jump + exact(carried[:, lanes], spread.astype(jnp.float32))
        state[:, lanes] = leaving
        carried[:, lanes] = jnp.broadcast_to(
            jnp.sum(leaving * entering, axis=0, keepdims=True), (8, LANES)
        )
        mixed = conv_of(extended, conv_value, conv_value_bias, lanes)
        sig = sigmoid(mixed)
        inner = grad_value * sig * (1.0 + mixed * (1.0 - sig))
        shifted[:SPAN, lanes] = inner
        grad_pre = jnp.zeros((SPAN, LANES), jnp.float32)
        for back in range(CONV):
            tap = conv_value[CONV - 1 - back : CONV - back, lanes]
            grad_pre = grad_pre + tap * shifted[back : back + SPAN, lanes]
            stat_out[CONV - 1 - back : CONV - back, lanes] += jnp.sum(
                inner * extended[EXTRA - back : EXTRA - back + SPAN, lanes], axis=0, keepdims=True
            )
        stat_out[CONV : CONV + 1, lanes] += jnp.sum(inner, axis=0, keepdims=True)
        stat_out[CONV + 1 : CONV + 2, lanes] += jnp.sum(value * upstream, axis=0, keepdims=True)
        grad_low = grad_pre.astype(jnp.bfloat16)
        value_out[:, lanes] = grad_low
        wide = grad_low.astype(jnp.float32)
        dots = dots + wide * extended[EXTRA:, lanes]
        stat_out[CONV + 2 : CONV + 3, lanes] = jnp.maximum(
            stat_out[CONV + 2 : CONV + 3, lanes], jnp.max(jnp.abs(wide), axis=0, keepdims=True)
        )
    high, low = split_bits(grad_scores)
    grad_inflow = grad_inflow + dot(high, readout) + dot(low, readout)
    high, low = split_bits(jnp.transpose(grad_scores))
    grad_readout = grad_readout + dot(high, inflow) + dot(low, inflow)
    part = select_out.shape[2]
    both = (grad_inflow, grad_readout)
    for index in range(select_out.shape[0]):
        start = index * part
        source = both[start // state_dim]
        select_out[index] = source[:, start % state_dim : start % state_dim + part]
    upper = (iota((SPAN, SPAN), 1) >= iota((SPAN, SPAN), 0)).astype(jnp.float32)
    flow = exact(upper, change) + jump[0:1, :]
    rate = -jnp.exp(decay_log[...])
    grad_delta = direct + rate * flow
    live = live_rows(fills[span], LANES)
    pre_step = step_pre[...]
    grad_step = grad_delta * live * sigmoid(pre_step + step_bias[...])
    grad_step = jnp.where(iota((SPAN, LANES), 1) < width // (LANES // 2), grad_step, 0.0)
    step_low = grad_step.astype(jnp.bfloat16)
    step_out[...] = step_low
    wide = step_low.astype(jnp.float32)
    dots = dots + wide * pre_step
    small_out[0:1, :] += jnp.sum(grad_step, axis=0, keepdims=True)
    small_out[1:2, :] += rate * jnp.sum(delta * flow, axis=0, keepdims=True)
    small_out[2:3, :] = jnp.maximum(small_out[2:3, :], jnp.max(jnp.abs(wide), axis=0, keepdims=True))
    rows_out[...] = above(row_of(dots), jnp.zeros((7, SPAN), jnp.float32))


def run_backward(starts, fills, tiles, states, vectors, parts):
    grad_scan, scan, values, value_pre, selects, delta, sums, step_pre = tiles
    rows, width = value_pre.shape
    spans = rows // SPAN
    select_width = selects.shape[1]

    def tile(columns):
        return pl.BlockSpec((SPAN, columns), lambda i: (spans - 1 - i, 0))

    before = pl.BlockSpec(
        (EXTRA, width), lambda i: (jnp.maximum((spans - 1 - i) * (SPAN // EXTRA) - 1, 0), 0)
    )
    return pl.pallas_call(
        functools.partial(backward_kernel, spans=spans),
        grid=(spans,),
        in_specs=[
            scalars(),
            scalars(),
            tile(width),
            tile(width),
            tile(width),
            tile(width),
            before,
            tile(select_width),
            tile(LANES),
            tile(LANES),
            tile(LANES),
            pl.BlockSpec((1, select_width // 2, width), lambda i: (spans - 1 - i, 0, 0)),
        ]
        + [fixed(array.shape) for array in vectors],
        out_specs=[
            tile(width),
            pl.BlockSpec((parts, SPAN, select_width // parts), lambda i: (0, spans - 1 - i, 0)),
            tile(LANES),
            pl.BlockSpec((8, SPAN), lambda i: (0, spans - 1 - i)),
            fixed((8, width)),
            fixed((8, LANES)),
        ],
        out_shape=[
            jax.ShapeDtypeStruct((rows, width), jnp.bfloat16),
            jax.ShapeDtypeStruct((parts, rows, select_width // parts), jnp.float32),
            jax.ShapeDtypeStruct((rows, LANES), jnp.bfloat16),
            jax.ShapeDtypeStruct((8, rows), jnp.float32),
            jax.ShapeDtypeStruct((8, width), jnp.float32),
            jax.ShapeDtypeStruct((8, LANES), jnp.float32),
        ],
        scratch_shapes=[
            pltpu.VMEM((SPAN + EXTRA, width), jnp.float32),
            pltpu.VMEM((SPAN + EXTRA, width), jnp.float32),
            pltpu.VMEM((select_width // 2, width), jnp.float32),
            pltpu.VMEM((8, width), jnp.float32),
        ],
        compiler_params=settings(52),
        name="backward",
    )(
        starts,
        fills,
        grad_scan,
        scan,
        values,
        value_pre,
        value_pre,
        selects,
        delta,
        sums,
        step_pre,
        states,
        *vectors,
    )


def exponent_of(bound):
    return jnp.ceil(jnp.log2(jnp.maximum(bound, 1e-30)) + 0.01)


def narrow(values, exponent):
    low = (values * jnp.exp2(TOP - exponent)).astype(jnp.float16)
    mark = jnp.broadcast_to(exponent.astype(jnp.float16), (EXTRA, low.shape[1]))
    return jnp.concatenate([low, mark], axis=0)


def mark_of(packet):
    return packet[-1, 0].astype(jnp.float32)


def pair_of(size):
    return [(spot, spot ^ 1) for spot in range(size)]


def shift_of(size, hops):
    groups = size // 2
    return [(spot, ((spot // 2 + hops) % groups) * 2 + spot % 2) for spot in range(size)]


def reduce_tokens(split, gradient, bound):
    size = lax.axis_size("dp")
    groups = size // 2
    piece = split.shape[2] // groups
    mine = lax.axis_index("dp") // 2
    exponent = exponent_of(bound)
    came = lax.ppermute(
        narrow(contract_rows(split[0], gradient), exponent), "dp", pair_of(size)
    )
    ours = contract_rows(split[1], gradient)
    other = mark_of(came)
    widening = jnp.exp2(other - TOP)
    exponent = jnp.maximum(exponent, other) + 1.0

    def both(place):
        start = place * piece
        added = lax.dynamic_slice_in_dim(came, start, piece, 0).astype(jnp.float32) * widening
        return lax.dynamic_slice_in_dim(ours, start, piece, 0) + added

    total = both(mine)
    arrived = [
        lax.ppermute(narrow(both((mine + hops) % groups), exponent), "dp", shift_of(size, hops))
        for hops in range(1, groups)
    ]
    for packet in arrived:
        total = total + packet[:piece].astype(jnp.float32) * jnp.exp2(mark_of(packet) - TOP)
    return total


def pick(stacked, place):
    return lax.dynamic_index_in_dim(stacked, place, 0, keepdims=False)


def scatter_plain(theirs, ours, axis, wire):
    size = lax.axis_size(axis)
    groups = size // 2
    mine = lax.axis_index(axis) // 2
    came = lax.ppermute(theirs, axis, pair_of(size))
    total = pick(ours, mine) + pick(came, mine)
    arrived = []
    for hops in range(1, groups):
        place = (mine + hops) % groups
        piece = (pick(ours, place) + pick(came, place)).astype(wire)
        arrived.append(lax.ppermute(piece, axis, shift_of(size, hops)))
    for piece in arrived:
        total = total + piece.astype(jnp.float32)
    return total


def features_kernel(place, gate, value, small, w_gate, w_value, w_small, out):
    total = dot_lanes(gate[...], w_gate[...])
    total = total + dot_lanes(value[...], w_value[...])
    out[0] = total + dot_lanes(small[...], w_small[...])


def back_features(place, gradients, weights, groups):
    rows = gradients[0].shape[0]
    features = weights[0].shape[0]
    piece = features // (2 * groups)
    return pl.pallas_call(
        features_kernel,
        grid_spec=pltpu.PrefetchScalarGridSpec(
            num_scalar_prefetch=1,
            grid=(groups, rows // 512),
            in_specs=[pl.BlockSpec((512, array.shape[1]), lambda g, t, at: (t, 0)) for array in gradients]
            + [
                pl.BlockSpec((piece, array.shape[1]), lambda g, t, at: (2 * g + at[0], 0))
                for array in weights
            ],
            out_specs=pl.BlockSpec((1, 512, piece), lambda g, t, at: (g, t, 0)),
        ),
        out_shape=jax.ShapeDtypeStruct((groups, rows, piece), jnp.float32),
        compiler_params=settings(40, 2),
        name="features",
    )(place, *gradients, *weights)


def sum_all(values, axis):
    size = lax.axis_size(axis)
    step = 1
    while step < size:
        values = values + lax.ppermute(values, axis, [(spot, spot ^ step) for spot in range(size)])
        step *= 2
    return values


def pack(arrays):
    flat = jnp.concatenate([array.reshape(-1) for array in arrays])
    length = flat.shape[0]
    whole = -(-length // 1024) * 1024
    return jnp.pad(flat, (0, whole - length)).reshape(whole // LANES, LANES)


def unpack(packed, likes):
    flat = packed.reshape(-1)
    out, start = [], 0
    for like in likes:
        count = like.size
        out.append(flat[start : start + count].reshape(like.shape))
        start += count
    return out


def layout(start_flags, token_rows):
    seq_numbers = jnp.repeat(jnp.cumsum(start_flags), SPAN, total_repeat_length=token_rows)
    same_links = []
    for back_steps in range(1, CONV):
        earlier = jnp.concatenate(
            [jnp.full((back_steps,), -1, jnp.int32), seq_numbers[:-back_steps]]
        )
        same_links.append((earlier == seq_numbers).astype(jnp.float32))
    return same_links


def conv_silu(pre_act, kernel, bias_vec, same_links):
    running_sum = bias_vec[None, :] + kernel[CONV - 1][None, :] * pre_act
    for back_steps in range(1, CONV):
        shifted = jnp.concatenate(
            [jnp.zeros((back_steps, pre_act.shape[1]), jnp.float32), pre_act[:-back_steps]], axis=0
        )
        running_sum = (
            running_sum
            + kernel[CONV - 1 - back_steps][None, :] * shifted * same_links[back_steps - 1][:, None]
        )
    return jax.nn.silu(running_sum)


def contract_rows(left_arr, right_arr):
    return lax.dot_general(
        left_arr, right_arr, (((0,), (0,)), ((), ())), preferred_element_type=jnp.float32
    )


def contract_cols(left_arr, right_arr):
    return lax.dot_general(
        left_arr, right_arr, (((1,), (1,)), ((), ())), preferred_element_type=jnp.float32
    )


def widen_lanes(vector):
    return jnp.pad(vector, (0, LANES - vector.shape[0]))[None, :]


def on_device(
    hidden_in,
    cotangent,
    span_starts,
    span_fill,
    norm_gain,
    w_gate,
    w_value,
    w_select,
    w_step,
    conv_value,
    conv_value_bias,
    conv_select,
    conv_select_bias,
    step_bias,
    decay_log,
    skip_gain,
    gate_gain,
    w_out,
):
    token_rows = hidden_in.shape[0]
    model_width = norm_gain.shape[0]
    inner_cols = w_gate.shape[1]
    local_heads = w_step.shape[1]
    head_dim = inner_cols // local_heads
    select_width = w_select.shape[1]
    model_parts = lax.axis_size("mp")
    model_groups = model_parts // 2
    data_parts = lax.axis_size("dp")
    inner_total = inner_cols * model_parts
    feature_piece = model_width // model_parts
    data_piece = model_width // data_parts
    part = select_width // model_parts
    model_spot = lax.axis_index("mp")
    model_side = model_spot % 2
    data_side = (lax.axis_index("dp") % 2).reshape(1)
    offset = model_spot * feature_piece
    select_start = model_spot * part

    gain_row = gate_gain[None, :]
    skip_row = jnp.repeat(skip_gain, head_dim, total_repeat_length=inner_cols)[None, :]
    bias_step = widen_lanes(step_bias)
    decay_row = widen_lanes(decay_log)
    wide_step = jnp.pad(w_step, ((0, 0), (0, LANES - local_heads)))
    own_select = lax.dynamic_slice_in_dim(w_select, select_start, part, 1)
    w_small = jnp.concatenate(
        [w_step, own_select, jnp.zeros((model_width, -(local_heads + part) % LANES), jnp.bfloat16)],
        axis=1,
    )

    whole_in = lax.all_gather(hidden_in, "mp", axis=1, tiled=True)
    whole_upstream = lax.all_gather(cotangent, "mp", axis=1, tiled=True)
    normed, normed_split, input_scale = normalize(whole_in, norm_gain[None, :], data_side, data_piece)
    gate_pre = jnp.dot(normed, w_gate, preferred_element_type=jnp.float32)
    value_pre = jnp.dot(normed, w_value, preferred_element_type=jnp.float32)
    step_pre = jnp.dot(normed, wide_step, preferred_element_type=jnp.float32)
    select_pre = jnp.dot(normed, w_select, preferred_element_type=jnp.float32)
    grad_scaled = contract_cols(whole_upstream, w_out)
    upstream_split = split_columns(whole_upstream, data_side, data_piece)

    values, selects, scan, delta, sums, states, row_part = run_forward(
        span_starts,
        span_fill,
        (value_pre, gate_pre, grad_scaled, select_pre, step_pre),
        (
            conv_value,
            conv_value_bias[None, :],
            conv_select,
            conv_select_bias[None, :],
            bias_step,
            decay_row,
            skip_row,
            gain_row,
        ),
    )
    row_sums = lax.psum(row_part, "mp")
    scaled, grad_gate, grad_scan, gate_rows, gate_stats = run_gate(
        span_fill, gate_pre, scan, grad_scaled, row_sums, gain_row, inner_total
    )
    scaled_bound = jnp.max(jnp.abs(gate_gain)) * (float(inner_total) ** 0.5 * token_rows)
    upstream_top = jnp.max(jnp.abs(whole_upstream)).astype(jnp.float32)
    grad_w_out = reduce_tokens(upstream_split, scaled, scaled_bound * upstream_top).T
    normed_bound = jnp.max(jnp.abs(norm_gain)) * (float(model_width) ** 0.5 * token_rows)
    grad_w_gate = reduce_tokens(normed_split, grad_gate, normed_bound * jnp.max(gate_stats[1]))
    mixed_share = lax.psum_scatter(
        jnp.dot(scaled, w_out, preferred_element_type=jnp.float32),
        "mp",
        scatter_dimension=1,
        tiled=True,
    )
    own_in = hidden_in.astype(jnp.float32)
    output = (own_in + mixed_share).astype(jnp.bfloat16)

    grad_value, select_parts, grad_step, value_rows, value_stats, small_stats = run_backward(
        span_starts,
        span_fill,
        (grad_scan, scan, values, value_pre, selects, delta, sums, step_pre),
        states,
        (conv_value, conv_value_bias[None, :], bias_step, decay_row, skip_row),
        model_parts,
    )
    grad_w_value = reduce_tokens(
        normed_split, grad_value, normed_bound * jnp.max(value_stats[CONV + 2])
    )
    same_links = layout(span_starts, token_rows)
    select_blocks = select_parts.reshape(model_groups, 2, token_rows, part)
    grad_selects = scatter_plain(
        lax.dynamic_index_in_dim(select_blocks, 1 - model_side, 1, keepdims=False),
        lax.dynamic_index_in_dim(select_blocks, model_side, 1, keepdims=False),
        "mp",
        jnp.float32,
    )
    select_own_pre = lax.dynamic_slice_in_dim(select_pre, select_start, part, 1)
    _, select_pull = jax.vjp(
        lambda pre_act, kernel, bias_vec: conv_silu(pre_act, kernel, bias_vec, same_links),
        select_own_pre,
        lax.dynamic_slice_in_dim(conv_select, select_start, part, 1),
        lax.dynamic_slice_in_dim(conv_select_bias, select_start, part, 0),
    )
    grad_select_pre, grad_conv_select_own, grad_conv_select_bias_own = select_pull(grad_selects)
    grad_select_low = grad_select_pre.astype(jnp.bfloat16)
    small_low = jnp.concatenate(
        [
            grad_step[:, :local_heads],
            grad_select_low,
            jnp.zeros((token_rows, -(local_heads + part) % LANES), jnp.bfloat16),
        ],
        axis=1,
    )
    small_top = jnp.maximum(
        jnp.max(small_stats[2]), jnp.max(jnp.abs(grad_select_low)).astype(jnp.float32)
    )
    grad_w_small = reduce_tokens(normed_split, small_low, normed_bound * small_top)
    grad_w_step = grad_w_small[:, :local_heads]
    grad_w_select = lax.all_gather(
        grad_w_small[:, local_heads : local_heads + part], "mp", axis=1, tiled=True
    )
    norm_dot = lax.psum(
        gate_rows[0]
        + value_rows[0]
        + jnp.sum(grad_select_low.astype(jnp.float32) * select_own_pre, axis=1),
        "mp",
    )
    back = [
        back_features(
            spot.reshape(1), (grad_gate, grad_value, small_low), (w_gate, w_value, w_small), model_groups
        )
        for spot in (1 - model_side, model_side)
    ]
    grad_normed = scatter_plain(back[0], back[1], "mp", jnp.bfloat16)
    own_gain = lax.dynamic_slice_in_dim(norm_gain, offset, feature_piece, 0)
    own_scale = input_scale[:, :1]
    weighted_in = grad_normed * own_gain[None, :]
    grad_hidden_in = (
        cotangent.astype(jnp.float32)
        + weighted_in * own_scale
        - own_in * own_scale**2 * norm_dot[:, None] / model_width
    )
    grad_norm_gain = jnp.sum(grad_normed * own_in * own_scale, axis=0)
    place = jnp.zeros((CONV + 1, model_parts, part), jnp.float32)
    select_small = lax.dynamic_update_slice_in_dim(
        place,
        jnp.concatenate([grad_conv_select_own, grad_conv_select_bias_own[None, :]], axis=0)[:, None, :],
        model_spot,
        1,
    ).reshape(CONV + 1, -1)
    select_small = lax.psum(select_small, "mp")
    likes = (
        grad_norm_gain,
        value_stats[:CONV],
        value_stats[CONV],
        select_small[:CONV],
        select_small[CONV],
        small_stats[0, :local_heads],
        small_stats[1, :local_heads],
        jnp.sum(value_stats[CONV + 1].reshape(local_heads, head_dim), axis=1),
        gate_stats[0],
    )
    small_sums = unpack(sum_all(pack(likes), "dp"), likes)
    return (
        output,
        grad_hidden_in,
        small_sums[0],
        grad_w_gate,
        grad_w_value,
        grad_w_select,
        grad_w_step,
        small_sums[1],
        small_sums[2],
        small_sums[3],
        small_sums[4],
        small_sums[5],
        small_sums[6],
        small_sums[7],
        small_sums[8],
        grad_w_out,
    )


def solution(mesh):
    in_specs = (
        P("dp", "mp"),
        P("dp", "mp"),
        P("dp"),
        P("dp"),
        P(),
        P(None, "mp"),
        P(None, "mp"),
        P(),
        P(None, "mp"),
        P(None, "mp"),
        P("mp"),
        P(),
        P(),
        P("mp"),
        P("mp"),
        P("mp"),
        P("mp"),
        P("mp", None),
    )
    out_specs = (
        P("dp", "mp"),
        P("dp", "mp"),
        P("mp"),
        P("dp", "mp"),
        P("dp", "mp"),
        P("dp", None),
        P("dp", "mp"),
        P(None, "mp"),
        P("mp"),
        P(),
        P(),
        P("mp"),
        P("mp"),
        P("mp"),
        P("mp"),
        P("mp", "dp"),
    )
    return jax.shard_map(
        on_device, mesh=mesh, in_specs=in_specs, out_specs=out_specs, check_vma=False
    )
```

time: 1200 us -> 583 us (0.49)
  waiting for transfers between devices: 654 us -> 173 us
  matrix products: 290 us -> 63.3 us
  Pallas kernels: 0 us -> 86.4 us
  starting transfers between devices: 0.87 us -> 35.8 us
  other arithmetic: 85.6 us -> 55.9 us
  between operations: 15.4 us -> 31.5 us
    reduce_scatter x6 -> x0, waiting for transfers between devices: 603 us -> none  [the longest x1 153 us: on_device(): lax.psum_scatter(contract_rows(normed, grad_value_low), 'dp', scatter_dim...]
    dot_general x69 -> x1, matrix products: 187 us -> 1.22 us  [on_device(): step_pre = jnp.dot(normed, wide_step, preferred_element_type=jnp.float32)]
    ppermute x0 -> x23, waiting for transfers between devices: none -> 130 us  [the longest x12 69.5 us: reduce_tokens(): lax.ppermute(narrow(both((mine + hops) % groups), exponent), 'dp', shift_...]
    pallas_call x0 -> x7, Pallas kernels: none -> 86.4 us  [the longest x1 38.8 us: run_backward(): pl.pallas_call(functools.partial(backward_kernel, spans=spans), grid=(spa...]
    reshape x11 -> x4, local copies, waits for them, and re-layouts: 45.9 us -> 1.3 us  [the longest x2 1.21 us: unpack(): out.append(flat[start:start + count].reshape(like.shape))]
    ppermute x0 -> x23, starting transfers between devices: none -> 35.7 us  [the longest x12 26.3 us: reduce_tokens(): lax.ppermute(narrow(both((mine + hops) % groups), exponent), 'dp', shift_...]
    reduce_scatter x1, waiting for transfers between devices: 26.2 us -> 0.01 us  [on_device(): lax.psum_scatter(jnp.dot(scaled, w_out, preferred_element_type=jnp.float3...]
    dot_general x5 -> x1, matrix products: 29.4 us -> 10 us  [contract_cols(): lax.dot_general(left_arr, right_arr, (((1,), (1,)), ((), ())), preferred_...]
  transfers between devices with their start and end apart: 10 -> 26, of which waited for: 8 -> 9; matrix products, arithmetic and copies ran while one was open for 22% -> 26% of each run, Pallas kernels for 0% -> 10%
where the time goes in v1:
time: 583 us; the launch traced here: 574 us
  waiting for transfers between devices  173 us (30%)
  Pallas kernels  86.4 us (15%)
  local copies, waits for them, and re-layouts  82.4 us (14%)
  matrix products  63.3 us (11%)
  other arithmetic  55.9 us (10%)
  blocking collectives  46.2 us (8%)
  starting transfers between devices  35.8 us (6%)
  between operations  31.5 us (5%)
    ppermute x12, waiting for transfers between devices, reduce_tokens(): lax.ppermute(narrow(both((mine + hops) % groups), exponent), 'dp', shift_...  69.5 us
    ppermute x4, waiting for transfers between devices, reduce_tokens(): lax.ppermute(narrow(contract_rows(split[0], gradient), exponent), 'dp', p...  58 us
    pallas_call x1, Pallas kernels, run_backward(): pl.pallas_call(functools.partial(backward_kernel, spans=spans), grid=(spa...  38.8 us
    unnamed x142, local copies, waits for them, and re-layouts  34.6 us
    dot_general x8, matrix products, contract_rows(): lax.dot_general(left_arr, right_arr, (((0,), (0,)), ((), ())), preferred_...  31.9 us
    psum x1, blocking collectives, on_device(): lax.psum(gate_rows[0] + value_rows[0] + jnp.sum(grad_select_low.astype(jn...  30.1 us
    all_gather x1, waiting for transfers between devices, on_device(): whole_in = lax.all_gather(hidden_in, 'mp', axis=1, tiled=True)  26.7 us
    ppermute x12, starting transfers between devices, reduce_tokens(): lax.ppermute(narrow(both((mine + hops) % groups), exponent), 'dp', shift_...  26.3 us
  transfers between devices with their start and end apart: 26, of which 9 were waited for; matrix products, arithmetic and copies ran while one was open for 26% of the time, Pallas kernels for 10%

profile of v1, /device:TPU:0, one launch (start us, length us, event | category | flops | bytes accessed | tf_op | source)
XLA Modules:
  0.0 574.1 jit_solution(8780085240943164636)
XLA Ops:
  9.6 4.5 compare_select_fusion.2
  14.3 5.8 %select_select_fusion.1 = f32[1024]{0:T(1024)S(1)} fusion(pred[1024]{0:T(1024)(128)(4,1)S(1)} %get-tuple-element.145, pred[1024]{0:T(1024)(128)(4,1)S(1)} %get-tuple-element.144, pred[1024]{0:T(1024)(128)(4,1)S(1)} %get-tuple-element.143, pred[1024]{0:T(1024)(128)(4,1)S(1)} %get-tuple-element.142, pred[1024]{0:T(1024)(128)(4,1)S(1)} %get-tuple-element.141, ...), kind=kLoop, calls=%fused_computation.115 | loop fusion | flops 9216 | bytes 17444 | tf_op jit(solution)/shard_map/jit(_take)/gather | solution.py:843
  20.2 26.7 %all-gather.3.cloned.1.call-done.hidden = bf16[1024,2048]{1,0:T(8,128)(2,1)} async-done(((bf16[1024,512]{1,0:T(8,128)(2,1)}), bf16[1024,2048]{1,0:T(8,128)(2,1)}) %all-gather.3.cloned.1.call-update) | async-done | bytes 4194320 | tf_op jit(solution)/shard_map/all_gather | solution.py:853
  56.0 6.1 %fusion.45.gate_pre = f32[1024,1024]{1,0:T(8,128)} fusion(bf16[1024,2048]{1,0:T(8,128)(2,1)S(1)} %get-tuple-element.61, bf16[2048,1024]{1,0:T(8,128)(2,1)S(1)} %copy-done.2), kind=kOutput, calls=%fused_computation.145 | convolution fusion | flops 4294967296 | bytes 12582912 | tf_op jit(solution)/shard_map/dot_general | solution.py:856
  62.1 6.1 %fusion.46.value_pre.value_before = f32[1024,1024]{1,0:T(8,128)} fusion(bf16[1024,2048]{1,0:T(8,128)(2,1)S(1)} %get-tuple-element.61, bf16[2048,1024]{1,0:T(8,128)(2,1)S(1)} %copy-done.42), kind=kOutput, calls=%fused_computation.146 | convolution fusion | flops 4294967296 | bytes 12582912 | tf_op jit(solution)/shard_map/dot_general | solution.py:857
  68.3 14.7 %all-gather.5.cloned.1.call-done.block = bf16[1024,2048]{1,0:T(8,128)(2,1)} async-done(((bf16[1024,512]{1,0:T(8,128)(2,1)}), bf16[1024,2048]{1,0:T(8,128)(2,1)}) %all-gather.5.cloned.1.call-update) | async-done | bytes 4194320 | tf_op jit(solution)/shard_map/all_gather | solution.py:854
  82.9 10.0 %fusion.47.grad_scaled = f32[1024,1024]{1,0:T(8,128)} fusion(bf16[1024,2048]{1,0:T(8,128)(2,1)} %all-gather.5.cloned.1.call-done.block, bf16[1024,2048]{1,0:T(8,128)(2,1)} %param.39), kind=kOutput, calls=%fused_computation.147 | convolution fusion | flops 4294967296 | bytes 12582912 | tf_op jit(solution)/shard_map/dot_general | solution.py:794
  93.0 21.5 %forward.1 = (bf16[1024,1024]{1,0:T(8,128)(2,1)S(1)}, bf16[1024,256]{1,0:T(8,128)(2,1)S(1)}, f32[1024,1024]{1,0:T(8,128)}, f32[1024,128]{1,0:T(8,128)S(1)}, f32[...) custom-call(s32[4]{0:T(128)S(1)} %copy-done.34, s32[4]{0:T(128)S(1)} %copy-done.33, ...), custom_call_target="tpu_custom_call" | custom-call | tf_op jit(solution)/shard_map/forward/pallas_call | solution.py:271
  117.4 10.4 %psum.21.sums = f32[8,1024]{1,0:T(8,128)S(1)} all-reduce(f32[8,1024]{1,0:T(8,128)S(1)} %get-tuple-element.63), channel_id=1, replica_groups=mesh['dp'=8,'mp'=4] {'mp'}, use_global_device_ids=true, to_apply=%region_0.1 | all-reduce | flops 8192 | bytes 65536 | tf_op jit(solution)/shard_map/psum | solution.py:878
  130.0 7.7 %gate.1 = (bf16[1024,1024]{1,0:T(8,128)(2,1)S(1)}, bf16[1024,1024]{1,0:T(8,128)(2,1)S(1)}, f32[1024,1024]{1,0:T(8,128)S(1)}, f32[8,1024]{1,0:T(8,128)S(1)}, f32[8,1024]{1,0:T(8,128)S(1)}) custom-call(s32[4]{0:T(128)S(1)} %copy-done.33, f32[1024,1024]{1,0:T(8,128)S(1)} %copy-done.8, f32[1024,1024]{1,0:T(8,128)} %get-tuple-element.62.scan_in, ...), custom_call_target="tpu_custom_call" | custom-call | tf_op jit(solution)/shard_map/gate/pallas_call | solution.py:362
  142.4 6.7 %fusion.49 = f32[1024,2048]{1,0:T(8,128)} fusion(bf16[1024,1024]{1,0:T(8,128)(2,1)S(1)} %get-tuple-element.64, bf16[1024,2048]{1,0:T(8,128)(2,1)S(1)} %copy-done.66), kind=kOutput, calls=%fused_computation.149 | convolution fusion | flops 4294967296 | bytes 14680064 | tf_op jit(solution)/shard_map/dot_general | solution.py:888
  165.3 38.8 %backward.1 = (bf16[1024,1024]{1,0:T(8,128)(2,1)}, f32[4,1024,64]{2,1,0:T(8,128)}, bf16[1024,128]{1,0:T(8,128)(2,1)S(1)}, f32[8,1024]{1,0:T(8,128)S(1)}, f32[8,1024]{1,0:T(8,128)S(1)}, /*index=5*/f32[8,128]{1,0:T(8,128)S(1)}) custom-call(s32[4]{0:T(128)S(1)} %copy-done.34, s32[4]{0:T(128)S(1)} %copy-done.33, f32[1024,1024]{1,0:T(8,128)} %copy-done.16, ...), custom_call_target="tpu_custom_call" | custom-call | tf_op jit(solution)/shard_map/backward/pallas_call | solution.py:578
  208.0 5.9 %multiply_convert_fusion.2 = f16[1024,1024]{1,0:T(8,128)(2,1)} fusion(bf16[1024,1024]{1,0:T(8,128)(2,1)} %copy-done.9, f32[]{:T(128)S(6)} %exp2.209, bf16[2,1024,1024]{2,1,0:T(8,128)(2,1)} %copy-done.37), kind=kOutput, calls=%fused_computation.3 | convolution fusion | flops 2149580800 | bytes 6291460 | tf_op jit(solution)/shard_map/dot_general | solution.py:788
  225.7 5.9 %multiply_convert_fusion.1 = f16[1024,1024]{1,0:T(8,128)(2,1)} fusion(bf16[1024,1024]{1,0:T(8,128)(2,1)} %get-tuple-element.72.value, f32[]{:T(128)S(6)} %exp2.224, bf16[2,1024,1024]{2,1,0:T(8,128)(2,1)} %copy-done.37), kind=kOutput, calls=%fused_computation.2 | convolution fusion | flops 2149580800 | bytes 6291460 | tf_op jit(solution)/shard_map/dot_general | solution.py:788
  244.6 8.2 %features.3 = f32[2,1024,512]{2,1,0:T(8,128)} custom-call(s32[1]{0:T(128)} %bitcast.45.place, bf16[1024,1024]{1,0:T(8,128)(2,1)S(1)} %copy-done.10, bf16[1024,1024]{1,0:T(8,128)(2,1)S(1)} %copy-done.13, bf16[1024,128]{1,0:T(8,128)(2,1)S(1)} %maximum_maximum_fusion.1.small, bf16[2048,1024]{1,0:T(8,128)(2,1)S(1)} %copy-done.3, bf16[2048,1024]{1,0:T(8,128)(2,1)} %w_value.3, ...), custom_call_target="tpu_custom_call" | custom-call | tf_op jit(solution)/shard_map/features/pallas_call | solution.py:719
  260.0 4.4 fusion.15
  264.4 4.4 fusion.13
  268.8 4.3 fusion.6
  273.1 3.7 multiply_convert_fusion
  276.8 3.6 concatenate.112
  289.5 7.2 %features.2 = f32[2,1024,512]{2,1,0:T(8,128)S(1)} custom-call(s32[1]{0:T(128)} %bitcast.29.place, bf16[1024,1024]{1,0:T(8,128)(2,1)S(1)} %copy-done.12, bf16[1024,1024]{1,0:T(8,128)(2,1)S(1)} %copy-done.15, bf16[1024,128]{1,0:T(8,128)(2,1)S(1)} %maximum_maximum_fusion.1.small, bf16[2048,1024]{1,0:T(8,128)(2,1)S(1)} %copy-done.4, bf16[2048,1024]{1,0:T(8,128)(2,1)} %w_value.3, ...), custom_call_target="tpu_custom_call" | custom-call | tf_op jit(solution)/shard_map/features/pallas_call | solution.py:719
  304.2 58.0 %collective-permute-done.15 = f16[1032,128]{1,0:T(8,128)(2,1)S(1)} collective-permute-done((f16[1032,128]{1,0:T(8,128)(2,1)S(1)}, f16[1032,128]{1,0:T(8,128)(2,1)S(1)}, u32[]{:S(2)}, u32[]{:S(2)}) %collective-permute-start.15) | collective-permute-done | bytes 264224 | tf_op jit(solution)/shard_map/ppermute | solution.py:666
  363.5 3.7 collective-permute-start.18
  372.6 30.1 %all-reduce.32 = (f32[1024]{0:T(1024)S(1)}, f32[5,256]{1,0:T(8,128)S(1)}) all-reduce(f32[1024]{0:T(1024)S(1)} %add.554, f32[5,256]{1,0:T(8,128)S(1)} %reshape.438), channel_id=1, replica_groups=mesh['dp'=8,'mp'=4] {'mp'}, use_global_device_ids=true, to_apply=%region_4.5 | all-reduce | flops 2304 | bytes 18432 | tf_op jit(solution)/shard_map/psum | solution.py:940
  420.8 5.8 %all_gather.11 = f32[256,256]{0,1:T(8,128)S(1)} all-gather(f32[256,64]{0,1:T(8,128)S(1)} %copy.52), channel_id=1, replica_groups=mesh['dp'=8,'mp'=4] {'mp'}, dimensions={1}, use_global_device_ids=true | all-gather | bytes 327680 | tf_op jit(solution)/shard_map/all_gather | solution.py:937
  445.4 6.0 %collective-permute-start.13 = (f16[264,1024]{1,0:T(8,128)(2,1)}, f16[264,1024]{1,0:T(8,128)(2,1)}, u32[]{:S(2)}, u32[]{:S(2)}) collective-permute-start(f16[264,1024]{1,0:T(8,128)(2,1)} %concatenate.106), channel_id=1, source_target_pairs={{0,16},{4,20},{8,24},{12,28},{16,0},{20,4},{24,8},{28,12},{1,17},{... | collective-permute-start | bytes 1622024 | tf_op jit(solution)/shard_map/ppermute | solution.py:681
  453.2 29.3 %collective-permute-done.9 = f16[264,1024]{1,0:T(8,128)(2,1)} collective-permute-done((f16[264,1024]{1,0:T(8,128)(2,1)}, f16[264,1024]{1,0:T(8,128)(2,1)}, u32[]{:S(2)}, u32[]{:S(2)}) %collective-permute-start.9) | collective-permute-done | bytes 540704 | tf_op jit(solution)/shard_map/ppermute | solution.py:681
  484.5 3.9 collective-permute-start.22
  490.2 5.0 collective-permute-start.21
  495.2 4.6 fusion.5
  501.9 32.8 %collective-permute-done.13 = f16[264,1024]{1,0:T(8,128)(2,1)} collective-permute-done((f16[264,1024]{1,0:T(8,128)(2,1)}, f16[264,1024]{1,0:T(8,128)(2,1)}, u32[]{:S(2)}, u32[]{:S(2)}) %collective-permute-start.13) | collective-permute-done | bytes 540704 | tf_op jit(solution)/shard_map/ppermute | solution.py:681
  550.4 4.4 collective-permute-done.21
  (302 shorter events, 152.4 us)
Async XLA Ops:
  7.2 46.1 %copy-start = (bf16[2048,256]{1,0:T(8,128)(2,1)S(1)}, bf16[2048,256]{1,0:T(8,128)(2,1)}, u32[]{:S(2)}) copy-start(bf16[2048,256]{1,0:T(8,128)(2,1)} %param.29) | copy-start | bytes 3145732
  7.2 39.6 %copy-start.29 = (f32[2048]{0:T(1024)S(1)}, f32[2048]{0:T(1024)}, u32[]{:S(2)}) copy-start(f32[2048]{0:T(1024)} %param.26) | copy-start | bytes 24580
  7.3 39.6 %all-gather.3.cloned.1.call-start = ((), (), s32[]{:S(2)}) async-start(), calls=%async_computation.1 | async-start | bytes 5242880 | tf_op jit(solution)/shard_map/all_gather | solution.py:853
  8.0 75.0 %all-gather.5.cloned.1.call-start = ((), (), s32[]{:S(2)}) async-start(), calls=%async_computation.2 | async-start | bytes 5242880 | tf_op jit(solution)/shard_map/all_gather | solution.py:854
  8.7 486.4 %reduce-scatter.2.cloned.1.call-start = ((), (), s32[]{:S(2)}) async-start(), calls=%async_computation.3 | async-start | bytes 10485760 | tf_op jit(solution)/shard_map/reduce_scatter | solution.py:887
  53.3 39.7 %copy-start.19 = (f32[1024,128]{1,0:T(8,128)}, f32[1024,128]{1,0:T(8,128)S(1)}, u32[]{:S(2)}) copy-start(f32[1024,128]{1,0:T(8,128)S(1)} %fusion.33.step_pre) | copy-start | bytes 1572868
  206.4 15.1 %collective-permute-start = (f32[2,1024,64]{1,2,0:T(8,128)S(1)}, f32[2,1024,64]{1,2,0:T(8,128)S(1)}, u32[]{:S(2)}, u32[]{:S(2)}) collective-permute-start(f32[2,1024,64]{1,2,0:T(8,128)S(1)} %bitcast.190), channel_id=1, source_target_pairs={{0,1},{1,0},{2,3},{3,2},{4,5},{5,4},{6,7},{7,6},{8,9},{9,8},{10,11... | collective-permute-start | bytes 1572872 | tf_op jit(solution)/shard_map/ppermute | solution.py:697
  217.5 192.6 %collective-permute-start.7 = (f16[1032,1024]{1,0:T(8,128)(2,1)}, f16[1032,1024]{1,0:T(8,128)(2,1)}, u32[]{:S(2)}, u32[]{:S(2)}) collective-permute-start(f16[1032,1024]{1,0:T(8,128)(2,1)} %concatenate.100), channel_id=1, source_target_pairs={{0,4},{4,0},{8,12},{12,8},{16,20},{20,16},{24,28},{28,24},{1,5},{5... | collective-permute-start | bytes 6340616 | tf_op jit(solution)/shard_map/ppermute | solution.py:666
  224.3 14.3 %collective-permute-start.1 = (f32[1024,64]{1,0:T(8,128)}, f32[1024,64]{1,0:T(8,128)}, u32[]{:S(2)}, u32[]{:S(2)}) collective-permute-start(f32[1024,64]{1,0:T(8,128)} %bitcast_add_fusion.1), channel_id=1, source_target_pairs={{0,2},{1,3},{2,0},{3,1},{4,6},{5,7},{6,4},{7,5},{8,10},{9,11},{10,... | collective-permute-start | bytes 786440 | tf_op jit(solution)/shard_map/ppermute | solution.py:703
  235.3 183.4 %collective-permute-start.11 = (f16[1032,1024]{1,0:T(8,128)(2,1)}, f16[1032,1024]{1,0:T(8,128)(2,1)}, u32[]{:S(2)}, u32[]{:S(2)}) collective-permute-start(f16[1032,1024]{1,0:T(8,128)(2,1)} %concatenate.104), channel_id=1, source_target_pairs={{0,4},{4,0},{8,12},{12,8},{16,20},{20,16},{24,28},{28,24},{1,5},{5... | collective-permute-start | bytes 6340616 | tf_op jit(solution)/shard_map/ppermute | solution.py:666
  252.8 114.4 %collective-permute-start.2 = (f32[2,1024,512]{2,1,0:T(8,128)}, f32[2,1024,512]{2,1,0:T(8,128)}, u32[]{:S(2)}, u32[]{:S(2)}) collective-permute-start(f32[2,1024,512]{2,1,0:T(8,128)} %features.3), channel_id=1, source_target_pairs={{0,1},{1,0},{2,3},{3,2},{4,5},{5,4},{6,7},{7,6},{8,9},{9,8},{10,11... | collective-permute-start | bytes 12582920 | tf_op jit(solution)/shard_map/ppermute | solution.py:697
  280.5 149.5 %collective-permute-start.19 = (f16[1032,1024]{1,0:T(8,128)(2,1)}, f16[1032,1024]{1,0:T(8,128)(2,1)}, u32[]{:S(2)}, u32[]{:S(2)}) collective-permute-start(f16[1032,1024]{1,0:T(8,128)(2,1)} %concatenate.112), channel_id=1, source_target_pairs={{0,4},{4,0},{8,12},{12,8},{16,20},{20,16},{24,28},{28,24},{1,5},{5... | collective-permute-start | bytes 6340616 | tf_op jit(solution)/shard_map/ppermute | solution.py:666
  301.3 60.8 %collective-permute-start.15 = (f16[1032,128]{1,0:T(8,128)(2,1)S(1)}, f16[1032,128]{1,0:T(8,128)(2,1)S(1)}, u32[]{:S(2)}, u32[]{:S(2)}) collective-permute-start(f16[1032,128]{1,0:T(8,128)(2,1)S(1)} %concatenate.108), channel_id=1, source_target_pairs={{0,4},{4,0},{8,12},{12,8},{16,20},{20,16},{24,28},{28,24},{1,5},{5... | collective-permute-start | bytes 792584 | tf_op jit(solution)/shard_map/ppermute | solution.py:666
  363.5 7.4 %collective-permute-start.18 = (f16[264,128]{1,0:T(8,128)(2,1)S(1)}, f16[264,128]{1,0:T(8,128)(2,1)S(1)}, u32[]{:S(2)}, u32[]{:S(2)}) collective-permute-start(f16[264,128]{1,0:T(8,128)(2,1)S(1)} %concatenate.111), channel_id=1, source_target_pairs={{0,24},{4,28},{8,0},{12,4},{16,8},{20,12},{24,16},{28,20},{1,25},{... | collective-permute-start | bytes 202760 | tf_op jit(solution)/shard_map/ppermute | solution.py:681
  367.3 35.5 %collective-permute-start.17 = (f16[264,128]{1,0:T(8,128)(2,1)S(1)}, f16[264,128]{1,0:T(8,128)(2,1)S(1)}, u32[]{:S(2)}, u32[]{:S(2)}) collective-permute-start(f16[264,128]{1,0:T(8,128)(2,1)S(1)} %concatenate.110), channel_id=1, source_target_pairs={{0,16},{4,20},{8,24},{12,28},{16,0},{20,4},{24,8},{28,12},{1,17},{... | collective-permute-start | bytes 202760 | tf_op jit(solution)/shard_map/ppermute | solution.py:681
  370.9 119.3 %collective-permute-start.3 = (bf16[1024,512]{1,0:T(8,128)(2,1)}, bf16[1024,512]{1,0:T(8,128)(2,1)S(1)}, u32[]{:S(2)}, u32[]{:S(2)}) collective-permute-start(bf16[1024,512]{1,0:T(8,128)(2,1)} %fusion.29), channel_id=1, source_target_pairs={{0,2},{1,3},{2,0},{3,1},{4,6},{5,7},{6,4},{7,5},{8,10},{9,11},{10,... | collective-permute-start | bytes 3145736 | tf_op jit(solution)/shard_map/ppermute | solution.py:703
  402.7 6.1 %collective-permute-start.16 = (f16[264,128]{1,0:T(8,128)(2,1)S(1)}, f16[264,128]{1,0:T(8,128)(2,1)S(1)}, u32[]{:S(2)}, u32[]{:S(2)}) collective-permute-start(f16[264,128]{1,0:T(8,128)(2,1)S(1)} %concatenate.109), channel_id=1, source_target_pairs={{0,8},{4,12},{8,16},{12,20},{16,24},{20,28},{24,0},{28,4},{1,9},{5... | collective-permute-start | bytes 202760 | tf_op jit(solution)/shard_map/ppermute | solution.py:681
  415.9 29.5 %collective-permute-start.10 = (f16[264,1024]{1,0:T(8,128)(2,1)}, f16[264,1024]{1,0:T(8,128)(2,1)}, u32[]{:S(2)}, u32[]{:S(2)}) collective-permute-start(f16[264,1024]{1,0:T(8,128)(2,1)} %concatenate.103), channel_id=1, source_target_pairs={{0,24},{4,28},{8,0},{12,4},{16,8},{20,12},{24,16},{28,20},{1,25},{... | collective-permute-start | bytes 1622024 | tf_op jit(solution)/shard_map/ppermute | solution.py:681
  417.0 65.5 %collective-permute-start.9 = (f16[264,1024]{1,0:T(8,128)(2,1)}, f16[264,1024]{1,0:T(8,128)(2,1)}, u32[]{:S(2)}, u32[]{:S(2)}) collective-permute-start(f16[264,1024]{1,0:T(8,128)(2,1)} %concatenate.102), channel_id=1, source_target_pairs={{0,16},{4,20},{8,24},{12,28},{16,0},{20,4},{24,8},{28,12},{1,17},{... | collective-permute-start | bytes 1622024 | tf_op jit(solution)/shard_map/ppermute | solution.py:681
  418.7 65.8 %collective-permute-start.8 = (f16[264,1024]{1,0:T(8,128)(2,1)}, f16[264,1024]{1,0:T(8,128)(2,1)}, u32[]{:S(2)}, u32[]{:S(2)}) collective-permute-start(f16[264,1024]{1,0:T(8,128)(2,1)} %concatenate.101), channel_id=1, source_target_pairs={{0,8},{4,12},{8,16},{12,20},{16,24},{20,28},{24,0},{28,4},{1,9},{5... | collective-permute-start | bytes 1622024 | tf_op jit(solution)/shard_map/ppermute | solution.py:681
  435.8 64.1 %collective-permute-start.14 = (f16[264,1024]{1,0:T(8,128)(2,1)}, f16[264,1024]{1,0:T(8,128)(2,1)}, u32[]{:S(2)}, u32[]{:S(2)}) collective-permute-start(f16[264,1024]{1,0:T(8,128)(2,1)} %concatenate.107), channel_id=1, source_target_pairs={{0,24},{4,28},{8,0},{12,4},{16,8},{20,12},{24,16},{28,20},{1,25},{... | collective-permute-start | bytes 1622024 | tf_op jit(solution)/shard_map/ppermute | solution.py:681
  442.6 52.6 %copy-start.43 = (bf16[1024,512]{1,0:T(8,128)(2,1)S(1)}, bf16[1024,512]{1,0:T(8,128)(2,1)}, u32[]{:S(2)}) copy-start(bf16[1024,512]{1,0:T(8,128)(2,1)} %param.22) | copy-start | bytes 3145732
  442.6 52.6 %copy-start.44 = (bf16[1024,512]{1,0:T(8,128)(2,1)S(1)}, bf16[1024,512]{1,0:T(8,128)(2,1)}, u32[]{:S(2)}) copy-start(bf16[1024,512]{1,0:T(8,128)(2,1)} %param.23) | copy-start | bytes 3145732
  442.6 52.6 %copy-start.52 = (f32[512]{0:T(512)S(1)}, f32[512]{0:T(512)}, u32[]{:S(2)}) copy-start(f32[512]{0:T(512)} %dynamic_slice.155) | copy-start | bytes 6148
  445.4 89.4 %collective-permute-start.13 = (f16[264,1024]{1,0:T(8,128)(2,1)}, f16[264,1024]{1,0:T(8,128)(2,1)}, u32[]{:S(2)}, u32[]{:S(2)}) collective-permute-start(f16[264,1024]{1,0:T(8,128)(2,1)} %concatenate.106), channel_id=1, source_target_pairs={{0,16},{4,20},{8,24},{12,28},{16,0},{20,4},{24,8},{28,12},{1,17},{... | collective-permute-start | bytes 1622024 | tf_op jit(solution)/shard_map/ppermute | solution.py:681
  482.6 60.7 %collective-permute-start.12 = (f16[264,1024]{1,0:T(8,128)(2,1)}, f16[264,1024]{1,0:T(8,128)(2,1)}, u32[]{:S(2)}, u32[]{:S(2)}) collective-permute-start(f16[264,1024]{1,0:T(8,128)(2,1)} %concatenate.105), channel_id=1, source_target_pairs={{0,8},{4,12},{8,16},{12,20},{16,24},{20,28},{24,0},{28,4},{1,9},{5... | collective-permute-start | bytes 1622024 | tf_op jit(solution)/shard_map/ppermute | solution.py:681
  484.5 64.1 %collective-permute-start.22 = (f16[264,1024]{1,0:T(8,128)(2,1)}, f16[264,1024]{1,0:T(8,128)(2,1)}, u32[]{:S(2)}, u32[]{:S(2)}) collective-permute-start(f16[264,1024]{1,0:T(8,128)(2,1)} %concatenate.115), channel_id=1, source_target_pairs={{0,24},{4,28},{8,0},{12,4},{16,8},{20,12},{24,16},{28,20},{1,25},{... | collective-permute-start | bytes 1622024 | tf_op jit(solution)/shard_map/ppermute | solution.py:681
  490.2 64.6 %collective-permute-start.21 = (f16[264,1024]{1,0:T(8,128)(2,1)}, f16[264,1024]{1,0:T(8,128)(2,1)}, u32[]{:S(2)}, u32[]{:S(2)}) collective-permute-start(f16[264,1024]{1,0:T(8,128)(2,1)} %concatenate.114), channel_id=1, source_target_pairs={{0,16},{4,20},{8,24},{12,28},{16,0},{20,4},{24,8},{28,12},{1,17},{... | collective-permute-start | bytes 1622024 | tf_op jit(solution)/shard_map/ppermute | solution.py:681
  499.9 56.9 %collective-permute-start.20 = (f16[264,1024]{1,0:T(8,128)(2,1)}, f16[264,1024]{1,0:T(8,128)(2,1)S(1)}, u32[]{:S(2)}, u32[]{:S(2)}) collective-permute-start(f16[264,1024]{1,0:T(8,128)(2,1)} %concatenate.113), channel_id=1, source_target_pairs={{0,8},{4,12},{8,16},{12,20},{16,24},{20,28},{24,0},{28,4},{1,9},{5... | collective-permute-start | bytes 1622024 | tf_op jit(solution)/shard_map/ppermute | solution.py:681
  534.7 10.4 %collective-permute-start.4 = (f32[64,128]{1,0:T(8,128)S(1)}, f32[64,128]{1,0:T(8,128)S(1)}, u32[]{:S(2)}, u32[]{:S(2)}) collective-permute-start(f32[64,128]{1,0:T(8,128)S(1)} %pad_bitcast_fusion), channel_id=1, source_target_pairs={{0,4},{4,0},{8,12},{12,8},{16,20},{20,16},{24,28},{28,24},{1,5},{5... | collective-permute-start | bytes 98312 | tf_op jit(solution)/shard_map/ppermute | solution.py:741
  545.2 12.8 %collective-permute-start.5 = (f32[64,128]{1,0:T(8,128)S(1)}, f32[64,128]{1,0:T(8,128)S(1)}, u32[]{:S(2)}, u32[]{:S(2)}) collective-permute-start(f32[64,128]{1,0:T(8,128)S(1)} %fusion.39), channel_id=1, source_target_pairs={{0,8},{4,12},{8,0},{12,4},{16,24},{20,28},{24,16},{28,20},{1,9},{5... | collective-permute-start | bytes 98312 | tf_op jit(solution)/shard_map/ppermute | solution.py:741
  558.0 4.9 collective-permute-start.6
  (61 other events, 387.7 us)
Sparse Core Ops, SparseCore 0:
  9.6 37.1 all-gather.2
  48.4 34.4 all-gather.4
  149.2 72.7 reduce-scatter.1
